TPU v7x, 256 devices: a whole 4x4x8 slice. The times are simulated.
256 devices in a mesh: grp: 4 (over y_lo, core), trk: 64 (over z, x, y_hi).
Axes of the slice: x: 4, y: 4 (y_hi: 2, y_lo: 2; y = y_hi * 2 + y_lo), z: 8, core: 2. Of those that a mesh axis runs over, the one named last changes fastest.
Arguments:
- fields: bfloat16 [256, 512, 512], P('grp', 'trk'), may hold values from -81 to 81
- upstream: bfloat16 [256, 512, 512], P('grp', 'trk'), may hold values from -6 to 6
- ln_gain: float32 [512], replicated, may hold values from 0.1 to 1.9
- weights: bfloat16 [4, 512, 512], P(None, 'grp', 'trk'), may hold values from -8 to 8
Outputs:
- grad_fields: bfloat16 [256, 512, 512], P('grp', 'trk')
- grad_weights: float32 [4, 512, 512], P(None, 'grp', 'trk')
- grad_gain: float32 [512], replicated
All inputs are finite; a program needn't handle non-finite values.
Results may differ from a plain program's by a relative error of at most 0.014.
The roundings to bfloat16 on the way count: a program that leaves them out, or rounds other values in their place, can miss the bound.
Values may be sent and summed in bfloat16 or wider, within the bound.
A program may use at most 64 MiB of HBM per device.

v0:
```python
import jax
import jax.numpy as jnp
from jax import lax
from jax.sharding import PartitionSpec as P

HEADS = 8


def normalize(fields, ln_gain):
    values = fields.astype(jnp.float32)
    row_mean = jnp.mean(values, -1, keepdims=True)
    offset = values - row_mean
    row_var = jnp.mean(offset * offset, -1, keepdims=True)
    inv_std = lax.rsqrt(row_var + 1e-05)
    centred = offset * inv_std
    normed = (centred * ln_gain).astype(jnp.bfloat16)
    return (normed, centred, inv_std)


def project(normed, w_in):
    return [
        jnp.einsum("rti,ij->rtj", normed, w_in[index], preferred_element_type=jnp.float32).astype(
            jnp.bfloat16
        )
        for index in range(3)
    ]


def split_heads(block, heads):
    rows, length, width = block.shape
    return (
        block.reshape(rows, length, heads, width // heads)
        .transpose(0, 2, 1, 3)
        .reshape(rows * heads, length, width // heads)
    )


def merge_heads(block, rows):
    items, length, size = block.shape
    return (
        block.reshape(rows, items // rows, length, size)
        .transpose(0, 2, 1, 3)
        .reshape(rows, length, items // rows * size)
    )


def head_back(members):
    query, keyed, valued, grad_out = members
    scaling = query.shape[-1] ** (-0.5)
    scores = jnp.einsum("qd,kd->qk", query, keyed, preferred_element_type=jnp.float32) * scaling
    row_max = jnp.max(scores, -1, keepdims=True)
    shifted = jnp.exp(scores - row_max)
    attn_prob = shifted / jnp.sum(shifted, -1, keepdims=True)
    prob_low = attn_prob.astype(jnp.bfloat16)
    output = jnp.einsum("qk,kd->qd", prob_low, valued, preferred_element_type=jnp.float32).astype(
        jnp.bfloat16
    )
    dprobs = jnp.einsum("qd,kd->qk", grad_out, valued, preferred_element_type=jnp.float32)
    row_dot = jnp.sum(attn_prob * dprobs, -1, keepdims=True)
    score_grad = (attn_prob * (dprobs - row_dot) * scaling).astype(jnp.bfloat16)
    grad_value = jnp.einsum(
        "qk,qd->kd", prob_low, grad_out, preferred_element_type=jnp.float32
    ).astype(jnp.bfloat16)
    grad_query = jnp.einsum(
        "qk,kd->qd", score_grad, keyed, preferred_element_type=jnp.float32
    ).astype(jnp.bfloat16)
    grad_key = jnp.einsum(
        "qk,qd->kd", score_grad, query, preferred_element_type=jnp.float32
    ).astype(jnp.bfloat16)
    return (output, grad_query, grad_key, grad_value)


def attend_back(query_proj, key_proj, value_proj, upstream_rows, w_out):
    rows = query_proj.shape[0]
    grad_attended = jnp.einsum(
        "rtj,ij->rti", upstream_rows, w_out, preferred_element_type=jnp.float32
    ).astype(jnp.bfloat16)
    pieces = lax.map(
        head_back,
        (
            split_heads(query_proj, HEADS),
            split_heads(key_proj, HEADS),
            split_heads(value_proj, HEADS),
            split_heads(grad_attended, HEADS),
        ),
    )
    return [merge_heads(piece, rows) for piece in pieces]


def input_grad(grad_query, grad_key, grad_value, w_in, centred, inv_std, ln_gain):
    stacked = jnp.stack([grad_query, grad_key, grad_value], 2)
    grad_normed = jnp.einsum("rtcj,cij->rti", stacked, w_in, preferred_element_type=jnp.float32)
    width = grad_normed.shape[-1]
    gain_term = jnp.sum((grad_normed * centred).reshape(-1, width), 0)
    scaled = grad_normed * ln_gain
    branch = inv_std * (
        scaled
        - jnp.mean(scaled, -1, keepdims=True)
        - centred * jnp.mean(scaled * centred, -1, keepdims=True)
    )
    return (branch.astype(jnp.bfloat16), gain_term)


def proj_grads(normed, grad_query, grad_key, grad_value):
    return [
        jnp.einsum("rti,rtj->ij", normed, member, preferred_element_type=jnp.float32)
        for member in (grad_query, grad_key, grad_value)
    ]


def shards(fields, upstream, ln_gain, weights):
    w_part = lax.all_gather(weights, "trk", axis=2, tiled=True)
    w_full = lax.all_gather(w_part, "grp", axis=1, tiled=True)
    w_in = w_full[:3]
    w_out = w_full[3]
    rows_dev, trk_dev, width = fields.shape
    cell_count = rows_dev * lax.axis_size("grp") * trk_dev * lax.axis_size("trk")
    normed, centred, inv_std = normalize(fields, ln_gain)
    query_proj, key_proj, value_proj = project(normed, w_in)
    query_rows, key_rows, value_rows, upstream_rows = (
        lax.all_to_all(query_proj, "trk", split_axis=0, concat_axis=1, tiled=True),
        lax.all_to_all(key_proj, "trk", split_axis=0, concat_axis=1, tiled=True),
        lax.all_to_all(value_proj, "trk", split_axis=0, concat_axis=1, tiled=True),
        lax.all_to_all(upstream, "trk", split_axis=0, concat_axis=1, tiled=True),
    )
    attended, grad_query, grad_key, grad_value = attend_back(
        query_rows, key_rows, value_rows, upstream_rows, w_out
    )
    back_query, back_key, back_value = (
        lax.all_to_all(grad_query, "trk", split_axis=1, concat_axis=0, tiled=True),
        lax.all_to_all(grad_key, "trk", split_axis=1, concat_axis=0, tiled=True),
        lax.all_to_all(grad_value, "trk", split_axis=1, concat_axis=0, tiled=True),
    )
    grad_list = proj_grads(normed, back_query, back_key, back_value)
    branch_cells, gain_term = input_grad(
        back_query, back_key, back_value, w_in, centred, inv_std, ln_gain
    )
    out_grad = jnp.einsum(
        "rti,rtj->ij", attended, upstream_rows, preferred_element_type=jnp.float32
    )
    raw_grad = jnp.stack(grad_list + [out_grad])
    partial_grad = lax.psum_scatter(
        raw_grad.astype(jnp.bfloat16), "grp", scatter_dimension=1, tiled=True
    ).astype(jnp.float32)
    summed_grad = lax.psum_scatter(partial_grad, "trk", scatter_dimension=2, tiled=True)
    gain_sum = lax.psum(gain_term, ("grp", "trk"))
    factor = float(cell_count) ** (-0.5)
    grad_fields = (upstream.astype(jnp.float32) + branch_cells.astype(jnp.float32)).astype(
        jnp.bfloat16
    )
    return (grad_fields, summed_grad * factor, gain_sum * factor)


def solution(mesh):
    in_specs = (P("grp", "trk", None), P("grp", "trk", None), P(), P(None, "grp", "trk"))
    out_specs = (P("grp", "trk", None), P(None, "grp", "trk"), P())
    return jax.shard_map(shards, mesh=mesh, in_specs=in_specs, out_specs=out_specs, check_vma=False)
```

profile of v0, /device:TPU:2, one launch (start us, length us, event | category | flops | bytes accessed | tf_op | source)
XLA Modules:
  0.0 1188.6 jit_solution(13073194801549360445)
XLA Ops:
  8.0 184.0 %all_gather.6 = bf16[4,128,512]{1,0,2:T(4,128)(2,1)S(1)} all-gather(bf16[4,128,8]{1,0,2:T(4,128)(2,1)S(1)} %copy.57), channel_id=1, replica_groups=mesh['grp'=4,'trk'=64] {'trk'}, dimensions={2}, use_global_device_ids=true | all-gather | bytes 532480 | tf_op jit(solution)/shard_map/all_gather | solution.py:112
  193.1 8.9 all-to-all-start.3
  202.5 21.9 %all-gather.2.cloned.1.call-done = bf16[4,512,512]{2,1,0:T(8,128)(2,1)} async-done(((bf16[4,128,512]{2,1,0:T(8,128)(2,1)}), bf16[4,512,512]{2,1,0:T(8,128)(2,1)}) %all-gather.2.cloned.1.call-update) | async-done | bytes 2097168 | tf_op jit(solution)/shard_map/all_gather | solution.py:113
  226.6 13.0 %all-to-all-start = ((bf16[64,8,512]{2,1,0:T(8,128)(2,1)}), bf16[64,8,512]{2,1,0:T(8,128)(2,1)S(1)}, u32[]{:S(2)}, u32[]{:S(2)}) async-start(bf16[64,8,512]{2,1,0:T(8,128)(2,1)} %convolution_convert_fusion.8), calls=%async_computation | async-start | bytes 1048576 | tf_op jit(solution)/shard_map/all_to_all | solution.py:121
  239.7 2.3 convolution_convert_fusion.7
  242.0 16.4 %all-to-all-done = bf16[64,8,512]{2,1,0:T(8,128)(2,1)S(1)} async-done(((bf16[64,8,512]{2,1,0:T(8,128)(2,1)}), bf16[64,8,512]{2,1,0:T(8,128)(2,1)S(1)}, u32[]{:S(2)}, u32[]{:S(2)}) %all-to-all-start) | async-done | bytes 524320 | tf_op jit(solution)/shard_map/all_to_all | solution.py:121
  258.4 6.5 all-to-all-start.1
  265.0 2.3 convolution_convert_fusion.6
  267.3 15.6 %all-to-all-done.1 = bf16[64,8,512]{2,1,0:T(8,128)(2,1)S(1)} async-done(((bf16[64,8,512]{2,1,0:T(8,128)(2,1)}), bf16[64,8,512]{2,1,0:T(8,128)(2,1)S(1)}, u32[]{:S(2)}, u32[]{:S(2)}) %all-to-all-start.1) | async-done | bytes 524320 | tf_op jit(solution)/shard_map/all_to_all | solution.py:122
  282.9 6.7 all-to-all-start.2
  293.1 2.4 reshape.122
  296.9 9.8 all-to-all-done.2
  306.7 2.4 reshape.124
  309.1 2.3 copy.62
  311.4 60.7 %while.16 = (s32[]{:T(128)}, bf16[8,512,64]{1,2,0:T(8,128)(2,1)}, bf16[8,512,64]{1,2,0:T(8,128)(2,1)}, bf16[8,512,64]{1,2,0:T(8,128)(2,1)}, bf16[8,512,64]{1,2,0...) while((s32[]{:T(128)}, bf16[8,512,64]{1,2,0:T(8,128)(2,1)}, ...), condition=%wide.region_6.7_spmd, body=%wide.region_2.6_spmd.sunk | while | flops 206699008 | bytes 11305061 | solution.py:78
  372.1 2.4 copy.65
  375.1 3.8 reduce.1
  379.9 6.5 all-to-all-start.6
  386.4 2.4 copy.64
  388.8 3.8 reduce.2
  393.6 9.5 all-to-all-done.6
  403.1 6.7 all-to-all-start.5
  409.8 2.4 copy.63
  412.2 3.8 reduce.3
  419.9 6.2 all-to-all-done.5
  426.1 6.6 all-to-all-start.4
  434.4 3.6 reshape.149
  439.5 8.9 all-to-all-done.4
  458.0 21.6 %reduce-scatter.2.cloned.1.call-done = bf16[4,128,512]{2,1,0:T(8,128)(2,1)} async-done(((bf16[4,512,512]{2,1,0:T(8,128)(2,1)}), bf16[4,128,512]{2,1,0:T(8,128)(2,1)}) %reduce-scatter.2.cloned.1.call-update) | async-done | bytes 524304 | tf_op jit(solution)/shard_map/reduce_scatter | solution.py:142
  481.9 2.8 fusion.64
  484.8 76.2 %psum.7 = f32[512]{0:T(512)S(1)} all-reduce(f32[512]{0:T(512)S(1)} %get-tuple-element.108), channel_id=1, replica_groups=mesh['grp'=4,'trk'=64] {'grp','trk'}, use_global_device_ids=true, to_apply=%region_12.13 | all-reduce | flops 512 | bytes 4096 | tf_op jit(solution)/shard_map/psum | solution.py:146
  562.8 617.9 %all-reduce.3.cloned.1.call-done = f32[4,128,512]{1,0,2:T(4,128)} async-done(((f32[4,128,512]{1,0,2:T(4,128)}), f32[4,128,512]{1,0,2:T(4,128)}) %all-reduce.3.cloned.1.call-update) | async-done | bytes 1048592
  (128 shorter events, 94.1 us)
Async XLA Ops:
  7.2 194.8 %copy-start = (bf16[64,8,512]{2,1,0:T(8,128)(2,1)S(1)}, bf16[64,8,512]{2,1,0:T(8,128)(2,1)}, u32[]{:S(2)}) copy-start(bf16[64,8,512]{2,1,0:T(8,128)(2,1)} %param.6) | copy-start | bytes 1572868
  7.2 217.1 %all-gather.2.cloned.1.call-start = ((), (), s32[]{:S(2)}) async-start(), calls=%async_computation.8 | async-start | bytes 2621440 | tf_op jit(solution)/shard_map/all_gather | solution.py:113
  8.0 216.3 %copy-start.8 = (f32[512]{0:T(512)S(1)}, f32[512]{0:T(512)}, u32[]{:S(2)}) copy-start(f32[512]{0:T(512)} %param.8) | copy-start | bytes 6148
  193.1 33.6 %all-to-all-start.3 = ((bf16[64,8,512]{2,1,0:T(8,128)(2,1)}), bf16[64,8,512]{2,1,0:T(8,128)(2,1)S(1)}, u32[]{:S(2)}, u32[]{:S(2)}) async-start(bf16[64,8,512]{2,1,0:T(8,128)(2,1)} %param.7), calls=%async_computation.3 | async-start | bytes 1048576 | tf_op jit(solution)/shard_map/all_to_all | solution.py:124
  226.6 31.8 %all-to-all-start = ((bf16[64,8,512]{2,1,0:T(8,128)(2,1)}), bf16[64,8,512]{2,1,0:T(8,128)(2,1)S(1)}, u32[]{:S(2)}, u32[]{:S(2)}) async-start(bf16[64,8,512]{2,1,0:T(8,128)(2,1)} %convolution_convert_fusion.8), calls=%async_computation | async-start | bytes 1048576 | tf_op jit(solution)/shard_map/all_to_all | solution.py:121
  258.4 24.4 %all-to-all-start.1 = ((bf16[64,8,512]{2,1,0:T(8,128)(2,1)}), bf16[64,8,512]{2,1,0:T(8,128)(2,1)S(1)}, u32[]{:S(2)}, u32[]{:S(2)}) async-start(bf16[64,8,512]{2,1,0:T(8,128)(2,1)} %convolution_convert_fusion.7), calls=%async_computation.1 | async-start | bytes 1048576 | tf_op jit(solution)/shard_map/all_to_all | solution.py:122
  282.9 9.6 copy-start.2
  282.9 23.8 %all-to-all-start.2 = ((bf16[64,8,512]{2,1,0:T(8,128)(2,1)}), bf16[64,8,512]{2,1,0:T(8,128)(2,1)}, u32[]{:S(2)}, u32[]{:S(2)}) async-start(bf16[64,8,512]{2,1,0:T(8,128)(2,1)} %convolution_convert_fusion.6), calls=%async_computation.2 | async-start | bytes 1048576 | tf_op jit(solution)/shard_map/all_to_all | solution.py:123
  379.9 23.2 %all-to-all-start.6 = ((bf16[64,2,2048]{2,1,0:T(2,128)(2,1)}), bf16[64,2,2048]{2,1,0:T(2,128)(2,1)S(1)}, u32[]{:S(2)}, u32[]{:S(2)}) async-start(bf16[64,2,2048]{2,1,0:T(2,128)(2,1)} %reshape.146), calls=%async_computation.6 | async-start | bytes 1048576 | tf_op jit(solution)/shard_map/all_to_all | solution.py:132
  403.1 22.9 %all-to-all-start.5 = ((bf16[64,2,2048]{2,1,0:T(2,128)(2,1)}), bf16[64,2,2048]{2,1,0:T(2,128)(2,1)}, u32[]{:S(2)}, u32[]{:S(2)}) async-start(bf16[64,2,2048]{2,1,0:T(2,128)(2,1)} %reshape.148), calls=%async_computation.5 | async-start | bytes 1048576 | tf_op jit(solution)/shard_map/all_to_all | solution.py:131
  426.1 22.4 %all-to-all-start.4 = ((bf16[64,2,2048]{2,1,0:T(2,128)(2,1)}), bf16[64,2,2048]{2,1,0:T(2,128)(2,1)S(1)}, u32[]{:S(2)}, u32[]{:S(2)}) async-start(bf16[64,2,2048]{2,1,0:T(2,128)(2,1)} %reshape.150), calls=%async_computation.4 | async-start | bytes 1048576 | tf_op jit(solution)/shard_map/all_to_all | solution.py:130
  432.6 47.0 %reduce-scatter.2.cloned.1.call-start = ((), (), s32[]{:S(2)}) async-start(), calls=%async_computation.9 | async-start | bytes 2621440 | tf_op jit(solution)/shard_map/reduce_scatter | solution.py:142
  450.2 2.0 copy-start.4
  450.2 2.0 copy-start.6
  450.2 2.0 copy-start.7
  453.9 0.7 copy-start.9
  453.9 726.9 %all-reduce.3.cloned.1.call-start = ((), (), s32[]{:S(2)}) async-start(), calls=%async_computation.10 | async-start | bytes 2097152
  455.8 1.3 copy-start.1
  457.1 24.8 %copy-start.5 = (bf16[1,512,512]{2,1,0:T(8,128)(2,1)S(1)}, bf16[1,512,512]{2,1,0:T(8,128)(2,1)}, u32[]{:S(2)}) copy-start(bf16[1,512,512]{2,1,0:T(8,128)(2,1)} %copy.94) | copy-start | bytes 1572868
  481.9 79.7 %copy-start.3 = (bf16[64,8,512]{2,1,0:T(8,128)(2,1)S(1)}, bf16[64,8,512]{2,1,0:T(8,128)(2,1)}, u32[]{:S(2)}) copy-start(bf16[64,8,512]{2,1,0:T(8,128)(2,1)} %param.7) | copy-start | bytes 1572868
Sparse Core Ops, SparseCore 0:
  193.2 31.0 all-gather.1
  454.0 25.5 reduce-scatter.1
  482.4 698.3 all-reduce.2
where the time goes:
time: 1190 us
  waiting for transfers between devices  728 us (61%)
  blocking collectives  260 us (22%)
  matrix products  75.3 us (6%)
  starting transfers between devices  55.3 us (5%)
  local copies, waits for them, and re-layouts  35.4 us (3%)
  other arithmetic  19.9 us (2%)
  between operations  14.7 us (1%)
    unnamed x4, waiting for transfers between devices  618 us
    all_gather x1, blocking collectives, shards(): w_part = lax.all_gather(weights, 'trk', axis=2, tiled=True)  184 us
    psum x1, blocking collectives, shards(): gain_sum = lax.psum(gain_term, ('grp', 'trk'))  76.2 us
  transfers between devices with their start and end apart: 10, of which 9 were waited for; matrix products, arithmetic and copies ran while one was open for 4% of the time, Pallas kernels for 0%

commit v1 on v0

v1 whole, which is shorter than its diff:
```python
import jax
import jax.numpy as jnp
from jax import lax
from jax.experimental import pallas as pl
from jax.experimental.pallas import tpu as pltpu
from jax.sharding import PartitionSpec as P

NZ, NX, NYH = 8, 4, 2
NYL, NC = 2, 2
HEAD = 64
MESH = pl.DeviceIdType.MESH
F32, BF16 = jnp.float32, jnp.bfloat16


def dot(a, b, ca, cb):
    return lax.dot_general(a, b, (((ca,), (cb,)), ((), ())), preferred_element_type=F32)


def position():
    grp, trk = lax.axis_index("grp"), lax.axis_index("trk")
    z, x, y_hi = trk // (NX * NYH), (trk // NYH) % NX, trk % NYH
    y_lo, core = grp // NC, grp % NC
    return grp, trk, z, x, y_hi, y_lo, core


def trk_of(z, x, y_hi):
    return (z * NX + x) * NYH + y_hi


def remote(src, dst, send, recv, grp, trk):
    return pltpu.make_async_remote_copy(
        src_ref=src, dst_ref=dst, send_sem=send, recv_sem=recv,
        device_id=(grp, trk), device_id_type=MESH,
    )


def enter(grp, trk, y_hi, y_lo, core, z, x):
    tracks = NZ * NX * NYH
    barrier = pltpu.get_barrier_semaphore()

    def greet(step, carry):
        pl.semaphore_signal(
            barrier, inc=1, device_id=(grp, lax.rem(trk + step, tracks)), device_id_type=MESH
        )
        return carry

    pl.semaphore_signal(barrier, inc=1, device_id=(y_lo * NC + 1 - core, trk), device_id_type=MESH)
    for far in range(NYH):
        pl.semaphore_signal(
            barrier,
            inc=1,
            device_id=((1 - y_lo) * NC + core, trk_of(z, x, (y_hi + far) % NYH)),
            device_id_type=MESH,
        )
    lax.fori_loop(1, tracks, greet, 0)
    pl.semaphore_wait(barrier, tracks - 1 + 1 + NYH)


def exchange_start(src, dst, send, recv, local, grp, trk):
    tracks = NZ * NX * NYH

    def send_one(step, carry):
        to = lax.rem(trk + step, tracks)
        remote(src.at[to], dst.at[trk], send, recv, grp, to).start()
        return carry

    lax.fori_loop(1, tracks, send_one, 0)
    pltpu.make_async_copy(src.at[trk], dst.at[trk], local).start()


def exchange_wait(src, dst, send, recv, local, grp, trk):
    tracks = NZ * NX * NYH
    rest = pl.ds(0, tracks - 1)
    whole = remote(src.at[rest], dst.at[rest], send, recv, grp, trk)
    whole.wait_recv()
    whole.wait_send()
    pltpu.make_async_copy(src.at[trk], dst.at[trk], local).wait()


def wait_all(view, send, recv, grp, trk):
    whole = remote(view, view, send, recv, grp, trk)
    whole.wait_send()
    whole.wait_recv()


def lanes(grp):
    return pl.ds(pl.multiple_of(grp * 128, 128), 128)


def gather_kernel(f_ref, u_ref, w_ref, fr_ref, ur_ref, wf_ref, send, recv, local):
    grp, trk, z, x, y_hi, y_lo, core = position()
    enter(grp, trk, y_hi, y_lo, core, z, x)
    mine = wf_ref.at[:, z, x, y_hi, :, lanes(grp)]
    own = pltpu.make_async_copy(w_ref, mine, local.at[2])
    own.start()
    along_z = [
        remote(w_ref, mine, send.at[2], recv.at[2], grp, trk_of((z + s) % NZ, x, y_hi))
        for s in range(1, NZ)
    ]
    for copy in along_z:
        copy.start()
    exchange_start(f_ref, fr_ref, send.at[0], recv.at[0], local.at[0], grp, trk)
    own.wait()
    wait_all(wf_ref.at[:, : NZ - 1, 0, 0, :, :128], send.at[2], recv.at[2], grp, trk)
    column = wf_ref.at[:, :, x, y_hi, :, lanes(grp)]
    along_x = [
        remote(column, column, send.at[3], recv.at[3], grp, trk_of(z, (x + s) % NX, y_hi))
        for s in range(1, NX)
    ]
    for copy in along_x:
        copy.start()
    exchange_start(u_ref, ur_ref, send.at[1], recv.at[1], local.at[1], grp, trk)
    wait_all(wf_ref.at[:, :, : NX - 1, 0, :, :128], send.at[3], recv.at[3], grp, trk)
    plane = wf_ref.at[:, :, :, y_hi, :, lanes(grp)]
    along_y = [
        remote(
            plane, plane, send.at[4], recv.at[4],
            ((y_lo + s % 2) % NYL) * NC + core, trk_of(z, x, (y_hi + s // 2) % NYH),
        )
        for s in range(1, NYL * NYH)
    ]
    for copy in along_y:
        copy.start()
    wait_all(wf_ref.at[:, :, :, 0, :, : (NYL * NYH - 1) * 128], send.at[4], recv.at[4], grp, trk)
    across = []
    for low in range(NYL):
        half = wf_ref.at[:, :, :, :, :, lanes(low * NC + core)]
        across.append(remote(half, half, send.at[5], recv.at[5], y_lo * NC + 1 - core, trk))
    for copy in across:
        copy.start()
    wait_all(wf_ref.at[:, :, :, :, :, : NYL * 128], send.at[5], recv.at[5], grp, trk)
    exchange_wait(f_ref, fr_ref, send.at[0], recv.at[0], local.at[0], grp, trk)
    exchange_wait(u_ref, ur_ref, send.at[1], recv.at[1], local.at[1], grp, trk)


def gather(fields, upstream, w_tile):
    tracks, cells, width = fields.shape
    rows = jax.ShapeDtypeStruct((tracks, cells, width), BF16)
    return pl.pallas_call(
        gather_kernel,
        out_shape=(
            rows,
            rows,
            jax.ShapeDtypeStruct((4, NZ, NX, NYH, w_tile.shape[1], width), BF16),
        ),
        in_specs=[pl.BlockSpec(memory_space=pl.ANY)] * 3,
        out_specs=[pl.BlockSpec(memory_space=pl.ANY)] * 3,
        scratch_shapes=[
            pltpu.SemaphoreType.DMA((6,)),
            pltpu.SemaphoreType.DMA((6,)),
            pltpu.SemaphoreType.DMA((3,)),
        ],
        compiler_params=pltpu.CompilerParams(collective_id=1, has_side_effects=True),
        name="gather_rows",
    )(fields, upstream, w_tile)


def row_kernel(
    f_ref, u_ref, w_ref, gain_ref, gf_ref, raw_ref, gg_ref,
    cen_ref, inv_ref, nor_ref, q_ref, k_ref, v_ref, ga_ref, at_ref, gq_ref, gk_ref, gv_ref,
):
    gain = gain_ref[...]
    values = f_ref[...].astype(F32)
    row_mean = jnp.mean(values, -1, keepdims=True)
    offset = values - row_mean
    inv_std = lax.rsqrt(jnp.mean(offset * offset, -1, keepdims=True) + 1e-05)
    centred = offset * inv_std
    cen_ref[...] = centred
    inv_ref[...] = inv_std
    nor_ref[...] = (centred * gain).astype(BF16)
    scaling = HEAD ** (-0.5)
    for index, ref in enumerate((q_ref, k_ref, v_ref)):
        ref[...] = dot(nor_ref[...], w_ref[index], 1, 1).astype(BF16)
    ga_ref[...] = dot(u_ref[...], w_ref[3], 1, 0).astype(BF16)
    width = f_ref.shape[1]
    length = f_ref.shape[0]
    half = length // 2
    lane = lax.broadcasted_iota(jnp.int32, (1, 128), 1)

    def pair(index, carry):
        cols = pl.ds(pl.multiple_of(index * 128, 128), 128)
        q, k, v, ga = q_ref[:, cols], k_ref[:, cols], v_ref[:, cols], ga_ref[:, cols]
        sum_k = jnp.zeros((length, 128), F32)
        sum_v = jnp.zeros((length, 128), F32)
        for part in range(2):
            rows = slice(part * half, (part + 1) * half)
            sum_o = jnp.zeros((half, 128), F32)
            sum_q = jnp.zeros((half, 128), F32)
            for head in range(2):
                mask = ((lane >= head * HEAD) & (lane < (head + 1) * HEAD)).astype(BF16)
                k_h, v_h = k * mask, v * mask
                q_h, ga_h = q[rows] * mask, ga[rows] * mask
                scores = dot(k_h, q[rows], 1, 1) * scaling
                shifted = jnp.exp(scores - jnp.max(scores, 0, keepdims=True))
                prob = shifted * (1.0 / jnp.sum(shifted, 0, keepdims=True))
                prob_low = prob.astype(BF16)
                dprobs = dot(v_h, ga[rows], 1, 1)
                row_dot = jnp.sum(prob * dprobs, 0, keepdims=True)
                grad = (prob * (dprobs - row_dot) * scaling).astype(BF16)
                sum_o += dot(prob_low, v_h, 0, 0)
                sum_q += dot(grad, k_h, 0, 0)
                sum_v += dot(prob_low, ga_h, 1, 0)
                sum_k += dot(grad, q_h, 1, 0)
            at_ref[rows, cols] = sum_o.astype(BF16)
            gq_ref[rows, cols] = sum_q.astype(BF16)
        gk_ref[:, cols] = sum_k.astype(BF16)
        gv_ref[:, cols] = sum_v.astype(BF16)
        return carry

    lax.fori_loop(0, width // 128, pair, 0)
    for index, ref in enumerate((gq_ref, gk_ref, gv_ref)):
        raw_ref[index] = dot(ref[...], nor_ref[...], 0, 0).astype(BF16)
    raw_ref[3] = dot(u_ref[...], at_ref[...], 0, 0).astype(BF16)
    grad_normed = (
        dot(gq_ref[...], w_ref[0], 1, 0)
        + dot(gk_ref[...], w_ref[1], 1, 0)
        + dot(gv_ref[...], w_ref[2], 1, 0)
    )
    centred = cen_ref[...]
    gg_ref[...] = jnp.sum(grad_normed * centred, 0, keepdims=True)
    scaled = grad_normed * gain
    branch = inv_ref[...] * (
        scaled
        - jnp.mean(scaled, -1, keepdims=True)
        - centred * jnp.mean(scaled * centred, -1, keepdims=True)
    )
    gf_ref[...] = (u_ref[...].astype(F32) + branch.astype(BF16).astype(F32)).astype(BF16)


def row_back(f_row, u_row, w_full, gain):
    length, width = f_row.shape
    square = pltpu.VMEM((length, width), BF16)
    return pl.pallas_call(
        row_kernel,
        out_shape=(
            jax.ShapeDtypeStruct((length, width), BF16),
            jax.ShapeDtypeStruct((4, width, width), BF16),
            jax.ShapeDtypeStruct((1, width), F32),
        ),
        in_specs=[pl.BlockSpec(memory_space=pltpu.VMEM)] * 4,
        out_specs=[pl.BlockSpec(memory_space=pltpu.VMEM)] * 3,
        scratch_shapes=[
            pltpu.VMEM((length, width), F32),
            pltpu.VMEM((length, 1), F32),
        ]
        + [square] * 9,
        compiler_params=pltpu.CompilerParams(vmem_limit_bytes=48 << 20),
        name="row_back",
    )(f_row, u_row, w_full, gain)


def scatter_kernel(
    gf_ref, raw_ref, gg_ref, out_ref, gw_ref, gain_ref,
    got_c, acc_c, got_y, acc_y, got_x, acc_x, got_z,
    sum_c, sum_y, sum_x, sum_z, send, recv, local,
):
    grp, trk, z, x, y_hi, y_lo, core = position()
    enter(grp, trk, y_hi, y_lo, core, z, x)
    other = y_lo * NC + 1 - core
    y_at = y_hi * NYL + y_lo

    swaps = []
    for low in range(NYL):
        theirs = raw_ref.at[:, :, :, :, :, lanes(low * NC + 1 - core)]
        swaps.append(remote(theirs, got_c.at[low], send.at[1], recv.at[1], other, trk))
    sum_c[core] = gg_ref[...]
    swaps.append(remote(gg_ref, sum_c.at[core], send.at[5], recv.at[5], other, trk))
    for copy in swaps:
        copy.start()
    exchange_start(gf_ref, out_ref, send.at[0], recv.at[0], local, grp, trk)
    wait_all(got_c, send.at[1], recv.at[1], grp, trk)
    wait_all(sum_c.at[0], send.at[5], recv.at[5], grp, trk)
    for low in range(NYL):
        acc_c[low] = (
            raw_ref[:, :, :, :, :, lanes(low * NC + core)].astype(F32) + got_c[low].astype(F32)
        ).astype(BF16)
    sum_y[y_at] = sum_c[0] + sum_c[1]

    def y_peer(s):
        return (y_lo + s % 2) % NYL, (y_hi + s // 2) % NYH

    swaps = []
    for s in range(1, NYL * NYH):
        low, high = y_peer(s)
        to = (low * NC + core, trk_of(z, x, high))
        swaps.append(
            remote(acc_c.at[low, :, :, :, high], got_y.at[y_at], send.at[2], recv.at[2], *to)
        )
        swaps.append(remote(sum_y.at[y_at], sum_y.at[y_at], send.at[6], recv.at[6], *to))
    for copy in swaps:
        copy.start()
    wait_all(got_y.at[: NYL * NYH - 1], send.at[2], recv.at[2], grp, trk)
    wait_all(sum_y.at[: NYL * NYH - 1], send.at[6], recv.at[6], grp, trk)
    total = acc_c[y_lo, :, :, :, y_hi].astype(F32)
    for s in range(1, NYL * NYH):
        low, high = y_peer(s)
        total += got_y[high * NYL + low].astype(F32)
    acc_y[...] = total.astype(BF16)
    sum_x[x] = sum_y[0] + sum_y[1] + sum_y[2] + sum_y[3]

    swaps = []
    for s in range(1, NX):
        at = (x + s) % NX
        to = (grp, trk_of(z, at, y_hi))
        swaps.append(remote(acc_y.at[:, :, at], got_x.at[x], send.at[3], recv.at[3], *to))
        swaps.append(remote(sum_x.at[x], sum_x.at[x], send.at[7], recv.at[7], *to))
    for copy in swaps:
        copy.start()
    wait_all(got_x.at[: NX - 1], send.at[3], recv.at[3], grp, trk)
    wait_all(sum_x.at[: NX - 1], send.at[7], recv.at[7], grp, trk)
    total = acc_y[:, :, x].astype(F32)
    for s in range(1, NX):
        total += got_x[(x + s) % NX].astype(F32)
    acc_x[...] = total.astype(BF16)
    all_x = sum_x[0]
    for s in range(1, NX):
        all_x += sum_x[s]
    sum_z[z] = all_x

    swaps = []
    for s in range(1, NZ):
        at = (z + s) % NZ
        to = (grp, trk_of(at, x, y_hi))
        swaps.append(remote(acc_x.at[:, at], got_z.at[z], send.at[4], recv.at[4], *to))
        swaps.append(remote(sum_z.at[z], sum_z.at[z], send.at[8], recv.at[8], *to))
    for copy in swaps:
        copy.start()
    wait_all(got_z.at[: NZ - 1], send.at[4], recv.at[4], grp, trk)
    wait_all(sum_z.at[: NZ - 1], send.at[8], recv.at[8], grp, trk)
    total = acc_x[:, z].astype(F32)
    for s in range(1, NZ):
        total += got_z[(z + s) % NZ].astype(F32)
    gw_ref[...] = total
    all_z = sum_z[0]
    for s in range(1, NZ):
        all_z += sum_z[s]
    gain_ref[...] = all_z
    exchange_wait(gf_ref, out_ref, send.at[0], recv.at[0], local, grp, trk)


def scatter(gf_row, raw, gain_term):
    tracks, cells, width = gf_row.shape
    outs = raw.shape[4]
    any_, vmem = pl.BlockSpec(memory_space=pl.ANY), pl.BlockSpec(memory_space=pltpu.VMEM)
    return pl.pallas_call(
        scatter_kernel,
        out_shape=(
            jax.ShapeDtypeStruct((tracks, cells, width), BF16),
            jax.ShapeDtypeStruct((4, outs, 128), F32),
            jax.ShapeDtypeStruct((1, width), F32),
        ),
        in_specs=[any_, vmem, vmem],
        out_specs=[any_, vmem, vmem],
        scratch_shapes=[
            pltpu.VMEM((NYL, 4, NZ, NX, NYH, outs, 128), BF16),
            pltpu.VMEM((NYL, 4, NZ, NX, NYH, outs, 128), BF16),
            pltpu.VMEM((NYL * NYH, 4, NZ, NX, outs, 128), BF16),
            pltpu.VMEM((4, NZ, NX, outs, 128), BF16),
            pltpu.VMEM((NX, 4, NZ, outs, 128), BF16),
            pltpu.VMEM((4, NZ, outs, 128), BF16),
            pltpu.VMEM((NZ, 4, outs, 128), BF16),
            pltpu.VMEM((NC, 1, width), F32),
            pltpu.VMEM((NYL * NYH, 1, width), F32),
            pltpu.VMEM((NX, 1, width), F32),
            pltpu.VMEM((NZ, 1, width), F32),
            pltpu.SemaphoreType.DMA((9,)),
            pltpu.SemaphoreType.DMA((9,)),
            pltpu.SemaphoreType.DMA,
        ],
        compiler_params=pltpu.CompilerParams(
            collective_id=2, has_side_effects=True, vmem_limit_bytes=32 << 20
        ),
        name="scatter_grads",
    )(gf_row, raw, gain_term)


def shards(fields, upstream, ln_gain, weights):
    tracks, cells, width = fields.shape
    cell_count = tracks * lax.axis_size("grp") * cells * lax.axis_size("trk")
    w_tile = jnp.swapaxes(weights, 1, 2)
    f_row, u_row, w_full = gather(fields, upstream, w_tile)
    gf_row, raw, gain_term = row_back(
        f_row.reshape(tracks * cells, width),
        u_row.reshape(tracks * cells, width),
        w_full.reshape(4, width, width),
        ln_gain.reshape(1, width),
    )
    grad_fields, raw_part, gain_sum = scatter(
        gf_row.reshape(tracks, cells, width),
        raw.reshape(4, NZ, NX, NYH, w_tile.shape[1], width),
        gain_term,
    )
    factor = float(cell_count) ** (-0.5)
    return (
        grad_fields,
        jnp.swapaxes(raw_part, 1, 2) * factor,
        gain_sum.reshape(width) * factor,
    )


def solution(mesh):
    in_specs = (P("grp", "trk", None), P("grp", "trk", None), P(), P(None, "grp", "trk"))
    out_specs = (P("grp", "trk", None), P(None, "grp", "trk"), P())
    return jax.shard_map(shards, mesh=mesh, in_specs=in_specs, out_specs=out_specs, check_vma=False)
```

time: 1190 us -> 106 us (0.09)
  waiting for transfers between devices: 728 us -> 0 us
  blocking collectives: 260 us -> 0 us
  Pallas kernels: 0 us -> 97.2 us
  matrix products: 75.3 us -> 0 us
  starting transfers between devices: 55.3 us -> 0 us
  local copies, waits for them, and re-layouts: 35.4 us -> 5.14 us
  other arithmetic: 19.9 us -> 1.19 us
  between operations: 14.7 us -> 0.67 us
    unnamed x4 -> x0, waiting for transfers between devices: 618 us -> none
    all_gather x1 -> x0, blocking collectives: 184 us -> none  [shards(): w_part = lax.all_gather(weights, 'trk', axis=2, tiled=True)]
    pallas_call x0 -> x3, Pallas kernels: none -> 97.2 us  [the longest x1 43.1 us: gather(): pl.pallas_call(gather_kernel, out_shape=(rows, rows, jax.ShapeDtypeStruct...]
    psum x1 -> x0, blocking collectives: 76.2 us -> none  [shards(): gain_sum = lax.psum(gain_term, ('grp', 'trk'))]
    dot_general x57 -> x0, matrix products: 75.3 us -> none  [the longest x8 14.8 us: head_back(): jnp.einsum('qk,qd->kd', prob_low, grad_out, preferred_element_type=jnp.fl...]
    all_to_all x7 -> x0, waiting for transfers between devices: 66.3 us -> none  [the longest x1 16.4 us: shards(): lax.all_to_all(query_proj, 'trk', split_axis=0, concat_axis=1, tiled=True)]
    all_to_all x7 -> x0, starting transfers between devices: 54.9 us -> none  [the longest x1 13 us: shards(): lax.all_to_all(query_proj, 'trk', split_axis=0, concat_axis=1, tiled=True)]
    all_gather x1 -> x0, waiting for transfers between devices: 21.9 us -> none  [shards(): w_full = lax.all_gather(w_part, 'grp', axis=1, tiled=True)]
  transfers between devices with their start and end apart: 10 -> 0, of which waited for: 9 -> 0; matrix products, arithmetic and copies ran while one was open for 4% -> 0% of each run, Pallas kernels for 0% -> 0%
where the time goes in v1:
time: 106 us; the launch traced here: 104 us
  Pallas kernels  97.2 us (92%)
  local copies, waits for them, and re-layouts  5.14 us (5%)
  other arithmetic  1.19 us (1%)
    pallas_call x1, Pallas kernels, gather(): pl.pallas_call(gather_kernel, out_shape=(rows, rows, jax.ShapeDtypeStruct...  43.1 us
    pallas_call x1, Pallas kernels, scatter(): pl.pallas_call(scatter_kernel, out_shape=(jax.ShapeDtypeStruct((tracks, c...  38.2 us
    pallas_call x1, Pallas kernels, row_back(): pl.pallas_call(row_kernel, out_shape=(jax.ShapeDtypeStruct((length, width...  15.9 us
    unnamed x9, local copies, waits for them, and re-layouts  5.14 us

profile of v1, /device:TPU:2, one launch (start us, length us, event | category | flops | bytes accessed | tf_op | source)
XLA Modules:
  0.0 104.2 jit_solution(1754773136909009211)
XLA Ops:
  0.6 43.1 %gather_rows.1 = (bf16[64,8,512]{2,1,0:T(8,128)(2,1)}, bf16[64,8,512]{2,1,0:T(8,128)(2,1)}, bf16[4,8,4,2,8,512]{5,4,3,2,1,0:T(8,128)(2,1)}) custom-call(bf16[64,8,512]{2,1,0:T(8,128)(2,1)} %f_ref.1, bf16[64,8,512]{2,1,0:T(8,128)(2,1)} %u_ref.1, bf16[4,8,128]{2,1,0:T(8,128)(2,1)} %bitcast.16), custom_call_target="tpu_custom_call" | custom-call | tf_op jit(solution)/shard_map/gather_rows/pallas_call | solution.py:139
  43.8 0.0 copy-start
  43.8 1.6 %copy-done = bf16[4,8,4,2,8,512]{5,4,3,2,1,0:T(8,128)(2,1)S(1)} copy-done((bf16[4,8,4,2,8,512]{5,4,3,2,1,0:T(8,128)(2,1)S(1)}, bf16[4,8,4,2,8,512]{5,4,3,2,1,0:T(8,128)(2,1)}, u32[]{:S(2)}) %copy-start) | copy-done | bytes 2097176
  45.4 0.0 copy-start.1
  45.4 1.0 copy-done.1
  46.4 0.0 copy-start.2
  46.4 1.0 copy-done.2
  47.5 0.0 copy-start.3
  47.5 0.7 copy-done.3
  48.1 15.9 %row_back.1 = (bf16[512,512]{1,0:T(8,128)(2,1)S(1)}, bf16[4,512,512]{2,1,0:T(8,128)(2,1)S(1)}, f32[1,512]{1,0:T(1,128)S(1)}) custom-call(bf16[512,512]{1,0:T(8,128)(2,1)S(1)} %bitcast.13, bf16[512,512]{1,0:T(8,128)(2,1)S(1)} %bitcast.14, bf16[4,512,512]{2,1,0:T(8,128)(2,1)S(1)} %bitcast.11, f32[1,512]{1,0:T(1,128)S(1)} %bitcast.15), custom_call_target="tpu_custom_call" | custom-call | tf_op jit(solution)/shard_map/row_back/pallas_call | solution.py:233
  64.0 38.2 %scatter_grads.1 = (bf16[64,8,512]{2,1,0:T(8,128)(2,1)S(1)}, f32[4,8,128]{2,1,0:T(8,128)S(1)}, f32[1,512]{1,0:T(1,128)S(1)}) custom-call(bf16[64,8,512]{2,1,0:T(8,128)(2,1)S(1)} %bitcast.12, bf16[4,8,4,2,8,512]{5,4,3,2,1,0:T(8,128)(2,1)S(1)} %bitcast.10, f32[1,512]{1,0:T(1,128)S(1)} %get-tuple-element.17.gg_ref), custom_call_target="tpu_custom_call" | custom-call | tf_op jit(solution)/shard_map/scatter_grads/pallas_call | solution.py:345
  102.2 0.6 broadcast_multiply_fusion
  102.8 0.6 multiply_bitcast_fusion
  103.4 0.8 copy.8
Async XLA Ops:
  43.8 1.6 %copy-start = (bf16[4,8,4,2,8,512]{5,4,3,2,1,0:T(8,128)(2,1)S(1)}, bf16[4,8,4,2,8,512]{5,4,3,2,1,0:T(8,128)(2,1)}, u32[]{:S(2)}) copy-start(bf16[4,8,4,2,8,512]{5,4,3,2,1,0:T(8,128)(2,1)} %get-tuple-element.14) | copy-start | bytes 6291460
  45.4 1.0 copy-start.1
  46.4 1.0 copy-start.2
  47.5 0.7 copy-start.3

commit v2 on v0

v2 whole, which is shorter than its diff:
```python
import jax
import jax.numpy as jnp
from jax import lax
from jax.experimental import pallas as pl
from jax.experimental.pallas import tpu as pltpu
from jax.sharding import PartitionSpec as P

NZ, NX, NYH = 8, 4, 2
NYL, NC = 2, 2
HEAD = 64
MESH = pl.DeviceIdType.MESH
F32, BF16 = jnp.float32, jnp.bfloat16


def dot(a, b, ca, cb):
    return lax.dot_general(a, b, (((ca,), (cb,)), ((), ())), preferred_element_type=F32)


def position():
    grp, trk = lax.axis_index("grp"), lax.axis_index("trk")
    z, x, y_hi = trk // (NX * NYH), (trk // NYH) % NX, trk % NYH
    y_lo, core = grp // NC, grp % NC
    return grp, trk, z, x, y_hi, y_lo, core


def trk_of(z, x, y_hi):
    return (z * NX + x) * NYH + y_hi


def remote(src, dst, send, recv, grp, trk):
    return pltpu.make_async_remote_copy(
        src_ref=src, dst_ref=dst, send_sem=send, recv_sem=recv,
        device_id=(grp, trk), device_id_type=MESH,
    )


def landed(view, recv, grp, trk):
    remote(view, view, recv, recv, grp, trk).wait_recv()


def left(view, send, grp, trk):
    remote(view, view, send, send, grp, trk).wait_send()


def lanes(grp):
    return pl.ds(pl.multiple_of(grp * 128, 128), 128)


def flips(value, count, stride):
    bits = count.bit_length() - 1
    return [(1 - 2 * ((value // 2**b) % 2)) * (2**b * stride) for b in range(bits)]


def row_kernel(
    f_ref, u_ref, w_ref, gain_ref, out_ref, gw_ref, gg_ref,
    fr, ur, wf, wt, cen_ref, inv_ref, prob_ref,
    up, nor, qr, kr, vr, gar, atr, gqr, gkr, gvr, branch,
    raw, got_c, acc_c, got_y, acc_y, got_x, acc_x, got_z,
    sum_c, sum_y, sum_x, sum_z,
    near, local, send_a, recv_a, send_w, recv_w, send_g, recv_g, send_s, recv_s,
):
    grp, trk, z, x, y_hi, y_lo, core = position()
    tracks, cells, width = f_ref.shape
    length = tracks * cells
    plane = NX * NYH
    ny = NYL * NYH
    y_at = y_hi * NYL + y_lo
    sibling = y_lo * NC + 1 - core

    def y_peer(s):
        return (y_lo + s % 2) % NYL, (y_hi + s // 2) % NYH

    z_peers = [(grp, trk_of((z + s) % NZ, x, y_hi)) for s in range(1, NZ)]
    x_peers = [(grp, trk_of(z, (x + s) % NX, y_hi)) for s in range(1, NX)]
    y_peers = []
    for s in range(1, ny):
        low, high = y_peer(s)
        y_peers.append((low * NC + core, trk_of(z, x, high)))

    barrier = pltpu.get_barrier_semaphore()
    greeted = z_peers + x_peers + y_peers + [(sibling, trk)]
    for peer in greeted:
        pl.semaphore_signal(barrier, inc=1, device_id=peer, device_id_type=MESH)
    pl.semaphore_wait(barrier, len(greeted))

    mine = wf.at[:, z, x, y_hi, :, lanes(grp)]
    own = pltpu.make_async_copy(w_ref, mine, local.at[2])
    own.start()
    for peer in z_peers:
        remote(w_ref, mine, send_w.at[0], recv_w.at[0], *peer).start()

    for peer in x_peers:
        pl.semaphore_signal(near.at[0], inc=1, device_id=peer, device_id_type=MESH)
    pl.semaphore_wait(near.at[0], len(x_peers))
    pl.semaphore_signal(
        near.at[1], inc=1, device_id=(grp, trk_of(z, x, 1 - y_hi)), device_id_type=MESH
    )
    pl.semaphore_wait(near.at[1], 1)

    in_plane = flips(trk % plane, plane, 1)
    over_z = flips(z, NZ, plane)
    offsets = []
    for k in range(plane):
        offset = trk * 0
        for b, flip in enumerate(in_plane):
            if (k >> b) & 1:
                offset = offset + flip
        offsets.append(offset)

    def exchange(src, dst, at, first, last):
        def some(high, skip):
            base = trk
            for b, flip in enumerate(over_z):
                base = base + ((high // 2**b) % 2) * flip
            for k in range(skip, plane):
                to = base + offsets[k]
                remote(src.at[to], dst.at[trk], send_a.at[at], recv_a.at[at], grp, to).start()

        def step(high, carry):
            some(high, 0)
            return carry

        if first == 0:
            pltpu.make_async_copy(src.at[trk], dst.at[trk], local.at[min(at, 1)]).start()
            some(0, 1)
            first = 1
        lax.fori_loop(first, last, step, 0)

    def exchanged(src, dst, at):
        landed(dst.at[: tracks - 1], recv_a.at[at], grp, trk)
        pltpu.make_async_copy(src.at[trk], dst.at[trk], local.at[min(at, 1)]).wait()

    exchange(f_ref, fr, 0, 0, NZ // 4)
    own.wait()
    landed(wf.at[:, : NZ - 1, 0, 0, :, :128], recv_w.at[0], grp, trk)
    column = wf.at[:, :, x, y_hi, :, lanes(grp)]
    for peer in x_peers:
        remote(column, column, send_w.at[1], recv_w.at[1], *peer).start()
    exchange(f_ref, fr, 0, NZ // 4, NZ // 2)
    landed(wf.at[:, :, : NX - 1, 0, :, :128], recv_w.at[1], grp, trk)
    for m in range(4):
        part = wf.at[m, :, :, y_hi, :, lanes(grp)]
        for peer in y_peers:
            remote(part, part, send_w.at[2 + m], recv_w.at[2 + m], *peer).start()
    exchange(f_ref, fr, 0, NZ // 2, NZ)

    def swap_weights(m):
        landed(wf.at[m, :, :, 0, :, : (ny - 1) * 128], recv_w.at[2 + m], grp, trk)
        for low in range(NYL):
            half = wf.at[m, :, :, :, :, lanes(low * NC + core)]
            remote(half, half, send_w.at[6 + m], recv_w.at[6 + m], sibling, trk).start()

    def take_weights(m):
        landed(wf.at[m, :, :, :, :, : NYL * 128], recv_w.at[6 + m], grp, trk)
        wt[m] = wf[m].astype(F32).reshape(width, width).astype(BF16)

    for m in range(3):
        swap_weights(m)
    exchange(u_ref, ur, 1, 0, NZ)
    swap_weights(3)

    gain = gain_ref[...]
    exchanged(f_ref, fr, 0)
    values = fr[...].astype(F32).reshape(length, width)
    offset = values - jnp.mean(values, -1, keepdims=True)
    inv_std = lax.rsqrt(jnp.mean(offset * offset, -1, keepdims=True) + 1e-05)
    centred = offset * inv_std
    cen_ref[...] = centred
    inv_ref[...] = inv_std
    nor[...] = (centred * gain).astype(BF16)
    scaling = HEAD ** (-0.5)
    for m, ref in enumerate((qr, kr, vr)):
        take_weights(m)
        ref[...] = dot(nor[...], wt[m], 1, 1).astype(BF16)
    half = length // 2
    lane = lax.broadcasted_iota(jnp.int32, (1, 128), 1)
    masks = [((lane >= h * HEAD) & (lane < (h + 1) * HEAD)).astype(BF16) for h in range(2)]
    pairs = width // 128

    def forward(pair, carry):
        cols = lanes(pair)
        q, k, v = qr[:, cols], kr[:, cols], vr[:, cols]
        for part in range(2):
            rows = slice(part * half, (part + 1) * half)
            sum_o = jnp.zeros((half, 128), F32)
            for h in range(2):
                scores = dot(k * masks[h], q[rows], 1, 1) * scaling
                shifted = jnp.exp(scores - jnp.max(scores, 0, keepdims=True))
                prob = shifted * (1.0 / jnp.sum(shifted, 0, keepdims=True))
                prob_ref[2 * pair + h, part] = prob
                sum_o += dot(prob.astype(BF16), v * masks[h], 0, 0)
            atr[rows, cols] = sum_o.astype(BF16)
        return carry

    lax.fori_loop(0, pairs, forward, 0)

    def chunk(c):
        if c == 0:
            return slice(3, 4), slice(0, NZ)
        return slice(0, 3), slice((c - 1) * NZ // pairs, c * NZ // pairs)

    def core_start(c):
        ms, zs = chunk(c)
        for low in range(NYL):
            theirs = raw.at[ms, zs, :, :, :, lanes(low * NC + 1 - core)]
            remote(
                theirs, got_c.at[low, ms, zs], send_g.at[0, c], recv_g.at[0, c], sibling, trk
            ).start()

    def core_finish(c):
        ms, zs = chunk(c)
        landed(got_c.at[:, ms, zs], recv_g.at[0, c], grp, trk)
        for low in range(NYL):
            acc_c[low, ms, zs] = (
                raw[ms, zs, :, :, :, lanes(low * NC + core)].astype(F32)
                + got_c[low, ms, zs].astype(F32)
            ).astype(BF16)
        for s in range(1, ny):
            low, high = y_peer(s)
            remote(
                acc_c.at[low, ms, zs, :, high], got_y.at[y_at, ms, zs],
                send_g.at[1, c], recv_g.at[1, c], *y_peers[s - 1],
            ).start()

    def y_finish(c):
        ms, zs = chunk(c)
        landed(got_y.at[: ny - 1, ms, zs], recv_g.at[1, c], grp, trk)
        total = acc_c[y_lo, ms, zs, :, y_hi].astype(F32)
        for s in range(1, ny):
            low, high = y_peer(s)
            total += got_y[high * NYL + low, ms, zs].astype(F32)
        acc_y[ms, zs] = total.astype(BF16)
        for s in range(1, NX):
            remote(
                acc_y.at[ms, zs, (x + s) % NX], got_x.at[x, ms, zs],
                send_g.at[2, c], recv_g.at[2, c], *x_peers[s - 1],
            ).start()

    def x_finish(c):
        ms, zs = chunk(c)
        landed(got_x.at[: NX - 1, ms, zs], recv_g.at[2, c], grp, trk)
        total = acc_y[ms, zs, x].astype(F32)
        for s in range(1, NX):
            total += got_x[(x + s) % NX, ms, zs].astype(F32)
        acc_x[ms, zs] = total.astype(BF16)

    raw_tiles = raw.shape[2:]

    exchanged(u_ref, ur, 1)
    up[...] = ur[...].astype(F32).reshape(length, width).astype(BF16)
    take_weights(3)
    gar[...] = dot(up[...], wt[3], 1, 0).astype(BF16)
    raw[3] = dot(up[...], atr[...], 0, 0).reshape(raw.shape[1:]).astype(BF16)
    core_start(0)
    for pair in range(pairs):
        cols = slice(pair * 128, (pair + 1) * 128)
        q, k, v, ga = qr[:, cols], kr[:, cols], vr[:, cols], gar[:, cols]
        sum_k = jnp.zeros((length, 128), F32)
        sum_v = jnp.zeros((length, 128), F32)
        for part in range(2):
            rows = slice(part * half, (part + 1) * half)
            sum_q = jnp.zeros((half, 128), F32)
            for h in range(2):
                prob = prob_ref[2 * pair + h, part]
                dprobs = dot(v * masks[h], ga[rows], 1, 1)
                row_dot = jnp.sum(prob * dprobs, 0, keepdims=True)
                grad = (prob * (dprobs - row_dot) * scaling).astype(BF16)
                sum_q += dot(grad, k * masks[h], 0, 0)
                sum_v += dot(prob.astype(BF16), ga[rows] * masks[h], 1, 0)
                sum_k += dot(grad, q[rows] * masks[h], 1, 0)
            gqr[rows, cols] = sum_q.astype(BF16)
        gkr[:, cols] = sum_k.astype(BF16)
        gvr[:, cols] = sum_v.astype(BF16)
        zs = chunk(pair + 1)[1]
        for m, ref in enumerate((gqr, gkr, gvr)):
            piece = dot(ref[:, cols], nor[...], 0, 0)
            raw[m, zs] = piece.reshape((zs.stop - zs.start,) + raw_tiles).astype(BF16)
        core_start(pair + 1)
        core_finish(pair)
        if pair >= 1:
            y_finish(pair - 1)
        if pair >= 2:
            x_finish(pair - 2)
    grad_normed = (
        dot(gqr[...], wt[0], 1, 0) + dot(gkr[...], wt[1], 1, 0) + dot(gvr[...], wt[2], 1, 0)
    )
    centred = cen_ref[...]
    sum_c[core] = jnp.sum(grad_normed * centred, 0, keepdims=True)
    remote(sum_c.at[core], sum_c.at[core], send_s.at[0], recv_s.at[0], sibling, trk).start()
    core_finish(pairs)
    scaled = grad_normed * gain
    grad = inv_ref[...] * (
        scaled
        - jnp.mean(scaled, -1, keepdims=True)
        - centred * jnp.mean(scaled * centred, -1, keepdims=True)
    )
    branch[...] = grad.reshape(tracks, cells, width).astype(BF16)
    landed(sum_c.at[0], recv_s.at[0], grp, trk)
    sum_y[y_at] = sum_c[0] + sum_c[1]
    for peer in y_peers:
        remote(sum_y.at[y_at], sum_y.at[y_at], send_s.at[1], recv_s.at[1], *peer).start()
    exchange(branch, out_ref, 2, 0, NZ // 2)
    y_finish(pairs - 1)
    x_finish(pairs - 2)
    landed(sum_y.at[: ny - 1], recv_s.at[1], grp, trk)
    all_y = sum_y[0]
    for s in range(1, ny):
        all_y += sum_y[s]
    sum_x[x] = all_y
    for peer in x_peers:
        remote(sum_x.at[x], sum_x.at[x], send_s.at[2], recv_s.at[2], *peer).start()
    y_finish(pairs)
    exchange(branch, out_ref, 2, NZ // 2, NZ)
    x_finish(pairs - 1)
    x_finish(pairs)
    for s in range(1, NZ):
        remote(
            acc_x.at[:, (z + s) % NZ], got_z.at[z], send_g.at[3, 0], recv_g.at[3, 0],
            *z_peers[s - 1],
        ).start()
    landed(sum_x.at[: NX - 1], recv_s.at[2], grp, trk)
    all_x = sum_x[0]
    for s in range(1, NX):
        all_x += sum_x[s]
    sum_z[z] = all_x
    for peer in z_peers:
        remote(sum_z.at[z], sum_z.at[z], send_s.at[3], recv_s.at[3], *peer).start()
    landed(got_z.at[: NZ - 1], recv_g.at[3, 0], grp, trk)
    total = acc_x[:, z].astype(F32)
    for s in range(1, NZ):
        total += got_z[(z + s) % NZ].astype(F32)
    gw_ref[...] = total
    landed(sum_z.at[: NZ - 1], recv_s.at[3], grp, trk)
    all_z = sum_z[0]
    for s in range(1, NZ):
        all_z += sum_z[s]
    gg_ref[...] = all_z
    exchanged(branch, out_ref, 2)

    for at in range(3):
        left(out_ref.at[: tracks - 1], send_a.at[at], grp, trk)
    left(wf.at[:, : NZ - 1, 0, 0, :, :128], send_w.at[0], grp, trk)
    left(wf.at[:, :, : NX - 1, 0, :, :128], send_w.at[1], grp, trk)
    for m in range(4):
        left(wf.at[m, :, :, 0, :, : (ny - 1) * 128], send_w.at[2 + m], grp, trk)
        left(wf.at[m, :, :, :, :, : NYL * 128], send_w.at[6 + m], grp, trk)
    for c in range(pairs + 1):
        ms, zs = chunk(c)
        left(got_c.at[:, ms, zs], send_g.at[0, c], grp, trk)
        left(got_y.at[: ny - 1, ms, zs], send_g.at[1, c], grp, trk)
        left(got_x.at[: NX - 1, ms, zs], send_g.at[2, c], grp, trk)
    left(got_z.at[: NZ - 1], send_g.at[3, 0], grp, trk)
    left(sum_c.at[0], send_s.at[0], grp, trk)
    left(sum_y.at[: ny - 1], send_s.at[1], grp, trk)
    left(sum_x.at[: NX - 1], send_s.at[2], grp, trk)
    left(sum_z.at[: NZ - 1], send_s.at[3], grp, trk)


def layer_back(fields, upstream, w_tile, gain):
    tracks, cells, width = fields.shape
    outs = w_tile.shape[1]
    length = tracks * cells
    ny = NYL * NYH
    any_, vmem = pl.BlockSpec(memory_space=pl.ANY), pl.BlockSpec(memory_space=pltpu.VMEM)
    dma = pltpu.SemaphoreType.DMA
    square = pltpu.VMEM((length, width), BF16)
    row = pltpu.VMEM((tracks, cells, width), BF16)
    return pl.pallas_call(
        row_kernel,
        out_shape=(
            jax.ShapeDtypeStruct((tracks, cells, width), BF16),
            jax.ShapeDtypeStruct((4, outs, 128), F32),
            jax.ShapeDtypeStruct((1, width), F32),
        ),
        in_specs=[any_, any_, any_, vmem],
        out_specs=[any_, vmem, vmem],
        scratch_shapes=[
            row,
            row,
            pltpu.VMEM((4, NZ, NX, NYH, outs, width), BF16),
            pltpu.VMEM((4, width, width), BF16),
            pltpu.VMEM((length, width), F32),
            pltpu.VMEM((length, 1), F32),
            pltpu.VMEM((width // HEAD, 2, length, length // 2), F32),
        ]
        + [square] * 10
        + [
            row,
            pltpu.VMEM((4, NZ, NX, NYH, outs, width), BF16),
            pltpu.VMEM((NYL, 4, NZ, NX, NYH, outs, 128), BF16),
            pltpu.VMEM((NYL, 4, NZ, NX, NYH, outs, 128), BF16),
            pltpu.VMEM((ny, 4, NZ, NX, outs, 128), BF16),
            pltpu.VMEM((4, NZ, NX, outs, 128), BF16),
            pltpu.VMEM((NX, 4, NZ, outs, 128), BF16),
            pltpu.VMEM((4, NZ, outs, 128), BF16),
            pltpu.VMEM((NZ, 4, outs, 128), BF16),
            pltpu.VMEM((NC, 1, width), F32),
            pltpu.VMEM((ny, 1, width), F32),
            pltpu.VMEM((NX, 1, width), F32),
            pltpu.VMEM((NZ, 1, width), F32),
            pltpu.SemaphoreType.REGULAR((2,)),
            dma((3,)),
            dma((3,)),
            dma((3,)),
            dma((10,)),
            dma((10,)),
            dma((4, 5)),
            dma((4, 5)),
            dma((4,)),
            dma((4,)),
        ],
        compiler_params=pltpu.CompilerParams(
            collective_id=1, has_side_effects=True, vmem_limit_bytes=56 << 20
        ),
        name="layer_back",
    )(fields, upstream, w_tile, gain)


def shards(fields, upstream, ln_gain, weights):
    tracks, cells, width = fields.shape
    cell_count = tracks * lax.axis_size("grp") * cells * lax.axis_size("trk")
    w_tile = jnp.swapaxes(weights, 1, 2)
    branch, raw_part, gain_sum = layer_back(fields, upstream, w_tile, ln_gain.reshape(1, width))
    factor = float(cell_count) ** (-0.5)
    return (
        (upstream.astype(F32) + branch.astype(F32)).astype(BF16),
        jnp.swapaxes(raw_part, 1, 2) * factor,
        gain_sum.reshape(width) * factor,
    )


def solution(mesh):
    in_specs = (P("grp", "trk", None), P("grp", "trk", None), P(), P(None, "grp", "trk"))
    out_specs = (P("grp", "trk", None), P(None, "grp", "trk"), P())
    return jax.shard_map(shards, mesh=mesh, in_specs=in_specs, out_specs=out_specs, check_vma=False)
```

time: 1190 us -> 94.1 us (0.08)
  waiting for transfers between devices: 728 us -> 0 us
  blocking collectives: 260 us -> 0 us
  Pallas kernels: 0 us -> 89.4 us
  matrix products: 75.3 us -> 0 us
  starting transfers between devices: 55.3 us -> 0 us
  local copies, waits for them, and re-layouts: 35.4 us -> 0.01 us
  other arithmetic: 19.9 us -> 3.16 us
  between operations: 14.7 us -> 0.67 us
    unnamed x4 -> x0, waiting for transfers between devices: 618 us -> none
    all_gather x1 -> x0, blocking collectives: 184 us -> none  [shards(): w_part = lax.all_gather(weights, 'trk', axis=2, tiled=True)]
    pallas_call x0 -> x1, Pallas kernels: none -> 89.4 us  [layer_back(): pl.pallas_call(row_kernel, out_shape=(jax.ShapeDtypeStruct((tracks, cells...]
    psum x1 -> x0, blocking collectives: 76.2 us -> none  [shards(): gain_sum = lax.psum(gain_term, ('grp', 'trk'))]
    dot_general x57 -> x0, matrix products: 75.3 us -> none  [the longest x8 14.8 us: head_back(): jnp.einsum('qk,qd->kd', prob_low, grad_out, preferred_element_type=jnp.fl...]
    all_to_all x7 -> x0, waiting for transfers between devices: 66.3 us -> none  [the longest x1 16.4 us: shards(): lax.all_to_all(query_proj, 'trk', split_axis=0, concat_axis=1, tiled=True)]
    all_to_all x7 -> x0, starting transfers between devices: 54.9 us -> none  [the longest x1 13 us: shards(): lax.all_to_all(query_proj, 'trk', split_axis=0, concat_axis=1, tiled=True)]
    all_gather x1 -> x0, waiting for transfers between devices: 21.9 us -> none  [shards(): w_full = lax.all_gather(w_part, 'grp', axis=1, tiled=True)]
  transfers between devices with their start and end apart: 10 -> 0, of which waited for: 9 -> 0; matrix products, arithmetic and copies ran while one was open for 4% -> 0% of each run, Pallas kernels for 0% -> 0%
where the time goes in v2:
time: 94.1 us; the launch traced here: 93.2 us
  Pallas kernels  89.4 us (95%)
  other arithmetic  3.16 us (3%)
    pallas_call x1, Pallas kernels, layer_back(): pl.pallas_call(row_kernel, out_shape=(jax.ShapeDtypeStruct((tracks, cells...  89.4 us
    convert_element_type x1, other arithmetic, shards(): (upstream.astype(F32) + branch.astype(F32)).astype(BF16)  1.97 us

profile of v2, /device:TPU:2, one launch (start us, length us, event | category | flops | bytes accessed | tf_op | source)
XLA Modules:
  0.0 93.2 jit_solution(12334102414345236508)
XLA Ops:
  0.6 0.0 copy-start
  0.6 89.4 %layer_back.1 = (bf16[64,8,512]{2,1,0:T(8,128)(2,1)}, f32[4,8,128]{2,1,0:T(8,128)}, f32[1,512]{1,0:T(1,128)}) custom-call(bf16[64,8,512]{2,1,0:T(8,128)(2,1)} %f_ref.1, bf16[64,8,512]{2,1,0:T(8,128)(2,1)} %u_ref.1, bf16[4,8,128]{2,1,0:T(8,128)(2,1)} %bitcast.5, f32[1,512]{1,0:T(1,128)} %bitcast.6), custom_call_target="tpu_custom_call" | custom-call | tf_op jit(solution)/shard_map/layer_back/pallas_call | solution.py:368
  90.0 0.0 copy-done
  90.0 0.0 copy-start.2
  90.0 0.0 copy-start.1
  90.1 2.0 %add_convert_fusion = bf16[64,8,512]{2,1,0:T(8,128)(2,1)} fusion(bf16[64,8,512]{2,1,0:T(8,128)(2,1)} %get-tuple-element.6, bf16[64,8,512]{2,1,0:T(8,128)(2,1)S(1)} %copy-done), kind=kLoop, calls=%fused_computation | loop fusion | flops 1048576 | bytes 1572864 | tf_op jit(solution)/shard_map/convert_element_type | solution.py:426
  92.0 0.0 copy-done.2
  92.0 0.6 broadcast_multiply_fusion
  92.6 0.0 copy-done.1
  92.6 0.6 multiply_bitcast_fusion
Async XLA Ops:
  0.6 89.4 %copy-start = (bf16[64,8,512]{2,1,0:T(8,128)(2,1)S(1)}, bf16[64,8,512]{2,1,0:T(8,128)(2,1)}, u32[]{:S(2)}) copy-start(bf16[64,8,512]{2,1,0:T(8,128)(2,1)} %u_ref.1) | copy-start | bytes 1572868
  90.0 2.0 %copy-start.2 = (f32[1,512]{1,0:T(1,128)S(1)}, f32[1,512]{1,0:T(1,128)}, u32[]{:S(2)}) copy-start(f32[1,512]{1,0:T(1,128)} %get-tuple-element.8) | copy-start | bytes 6148
  90.0 2.6 %copy-start.1 = (f32[4,8,128]{2,1,0:T(8,128)S(1)}, f32[4,8,128]{2,1,0:T(8,128)}, u32[]{:S(2)}) copy-start(f32[4,8,128]{2,1,0:T(8,128)} %get-tuple-element.7) | copy-start | bytes 49156

commit v3 on v2

--- a/solution.py
+++ b/solution.py
@@ -53,11 +53,11 @@
 
 def row_kernel(
     f_ref, u_ref, w_ref, gain_ref, out_ref, gw_ref, gg_ref,
-    fr, ur, wf, wt, cen_ref, inv_ref, prob_ref,
+    fs, us, fr, ur, wf, wt, cen_ref, inv_ref, prob_ref,
     up, nor, qr, kr, vr, gar, atr, gqr, gkr, gvr, branch,
-    raw, got_c, acc_c, got_y, acc_y, got_x, acc_x, got_z,
+    raw, got_c, acc_c, got_y, acc_y, got_x, got_xf, acc_xf, got_yl, acc, got_z,
     sum_c, sum_y, sum_x, sum_z,
-    near, local, send_a, recv_a, send_w, recv_w, send_g, recv_g, send_s, recv_s,
+    local, send_a, recv_a, send_w, recv_w, send_g, recv_g, send_s, recv_s,
 ):
     grp, trk, z, x, y_hi, y_lo, core = position()
     tracks, cells, width = f_ref.shape
@@ -77,25 +77,34 @@
         low, high = y_peer(s)
         y_peers.append((low * NC + core, trk_of(z, x, high)))
 
-    barrier = pltpu.get_barrier_semaphore()
-    greeted = z_peers + x_peers + y_peers + [(sibling, trk)]
-    for peer in greeted:
-        pl.semaphore_signal(barrier, inc=1, device_id=peer, device_id_type=MESH)
-    pl.semaphore_wait(barrier, len(greeted))
-
+    loads = [
+        pltpu.make_async_copy(src, dst, local.at[3 + i])
+        for i, (src, dst) in enumerate(((f_ref, fs), (u_ref, us)))
+    ]
+    for load in loads:
+        load.start()
     mine = wf.at[:, z, x, y_hi, :, lanes(grp)]
     own = pltpu.make_async_copy(w_ref, mine, local.at[2])
     own.start()
+
+    barrier = pltpu.get_barrier_semaphore()
+
+    def greet(step, carry):
+        to = lax.rem(trk + tracks // 2 + step, tracks)
+        pl.semaphore_signal(barrier, inc=1, device_id=(grp, to), device_id_type=MESH)
+        return carry
+
+    lax.fori_loop(0, tracks // 2, greet, 0)
+    lax.fori_loop(tracks // 2 + 1, tracks, greet, 0)
+    for peer in y_peers:
+        pl.semaphore_signal(barrier, inc=1, device_id=peer, device_id_type=MESH)
+    pl.semaphore_signal(barrier, inc=1, device_id=(sibling, trk), device_id_type=MESH)
+    pl.semaphore_wait(barrier, tracks - 1 + len(y_peers) + 1)
+
     for peer in z_peers:
         remote(w_ref, mine, send_w.at[0], recv_w.at[0], *peer).start()
-
-    for peer in x_peers:
-        pl.semaphore_signal(near.at[0], inc=1, device_id=peer, device_id_type=MESH)
-    pl.semaphore_wait(near.at[0], len(x_peers))
-    pl.semaphore_signal(
-        near.at[1], inc=1, device_id=(grp, trk_of(z, x, 1 - y_hi)), device_id_type=MESH
-    )
-    pl.semaphore_wait(near.at[1], 1)
+    for load in loads:
+        load.wait()
 
     in_plane = flips(trk % plane, plane, 1)
     over_z = flips(z, NZ, plane)
@@ -130,22 +139,38 @@
         landed(dst.at[: tracks - 1], recv_a.at[at], grp, trk)
         pltpu.make_async_copy(src.at[trk], dst.at[trk], local.at[min(at, 1)]).wait()
 
-    exchange(f_ref, fr, 0, 0, NZ // 4)
+    exchange(fs, fr, 0, 0, NZ)
     own.wait()
     landed(wf.at[:, : NZ - 1, 0, 0, :, :128], recv_w.at[0], grp, trk)
-    column = wf.at[:, :, x, y_hi, :, lanes(grp)]
+    by_x = wf.at[:2, :, x, y_hi, :, lanes(grp)]
+    by_y = wf.at[2:, :, x, y_hi, :, lanes(grp)]
     for peer in x_peers:
-        remote(column, column, send_w.at[1], recv_w.at[1], *peer).start()
-    exchange(f_ref, fr, 0, NZ // 4, NZ // 2)
-    landed(wf.at[:, :, : NX - 1, 0, :, :128], recv_w.at[1], grp, trk)
-    for m in range(4):
-        part = wf.at[m, :, :, y_hi, :, lanes(grp)]
-        for peer in y_peers:
-            remote(part, part, send_w.at[2 + m], recv_w.at[2 + m], *peer).start()
-    exchange(f_ref, fr, 0, NZ // 2, NZ)
+        remote(by_x, by_x, send_w.at[1], recv_w.at[1], *peer).start()
+    for peer in y_peers:
+        remote(by_y, by_y, send_w.at[10], recv_w.at[10], *peer).start()
+    exchange(us, ur, 1, 0, NZ // 2)
+    landed(wf.at[:2, :, : NX - 1, 0, :, :128], recv_w.at[1], grp, trk)
+    landed(wf.at[2:, :, 0, 0, :, : (ny - 1) * 128], recv_w.at[10], grp, trk)
+    for m in (0, 2, 1, 3):
+        if m < 2:
+            part = wf.at[m, :, :, y_hi, :, lanes(grp)]
+            for peer in y_peers:
+                remote(part, part, send_w.at[2 + m], recv_w.at[2 + m], *peer).start()
+        else:
+            for s in range(ny):
+                low, high = y_peer(s)
+                part = wf.at[m, :, x, high, :, lanes(low * NC + core)]
+                for peer in x_peers:
+                    remote(part, part, send_w.at[2 + m], recv_w.at[2 + m], *peer).start()
+    exchange(us, ur, 1, NZ // 2, NZ)
+
+    def last_stage(m):
+        if m < 2:
+            return wf.at[m, :, :, 0, :, : (ny - 1) * 128]
+        return wf.at[m, :, : NX - 1, :, :, : ny // NYH * 128]
 
     def swap_weights(m):
-        landed(wf.at[m, :, :, 0, :, : (ny - 1) * 128], recv_w.at[2 + m], grp, trk)
+        landed(last_stage(m), recv_w.at[2 + m], grp, trk)
         for low in range(NYL):
             half = wf.at[m, :, :, :, :, lanes(low * NC + core)]
             remote(half, half, send_w.at[6 + m], recv_w.at[6 + m], sibling, trk).start()
@@ -154,13 +179,11 @@
         landed(wf.at[m, :, :, :, :, : NYL * 128], recv_w.at[6 + m], grp, trk)
         wt[m] = wf[m].astype(F32).reshape(width, width).astype(BF16)
 
-    for m in range(3):
+    for m in (0, 2, 1, 3):
         swap_weights(m)
-    exchange(u_ref, ur, 1, 0, NZ)
-    swap_weights(3)
 
     gain = gain_ref[...]
-    exchanged(f_ref, fr, 0)
+    exchanged(fs, fr, 0)
     values = fr[...].astype(F32).reshape(length, width)
     offset = values - jnp.mean(values, -1, keepdims=True)
     inv_std = lax.rsqrt(jnp.mean(offset * offset, -1, keepdims=True) + 1e-05)
@@ -169,7 +192,7 @@
     inv_ref[...] = inv_std
     nor[...] = (centred * gain).astype(BF16)
     scaling = HEAD ** (-0.5)
-    for m, ref in enumerate((qr, kr, vr)):
+    for m, ref in ((0, qr), (2, vr), (1, kr)):
         take_weights(m)
         ref[...] = dot(nor[...], wt[m], 1, 1).astype(BF16)
     half = length // 2
@@ -199,6 +222,12 @@
             return slice(3, 4), slice(0, NZ)
         return slice(0, 3), slice((c - 1) * NZ // pairs, c * NZ // pairs)
 
+    def y_first(c):
+        return c > 0, slice(0, 2), chunk(c)[1]
+
+    def x_first(c):
+        return slice(2, 3) if c > 0 else slice(3, 4), chunk(c)[1]
+
     def core_start(c):
         ms, zs = chunk(c)
         for low in range(NYL):
@@ -215,38 +244,67 @@
                 raw[ms, zs, :, :, :, lanes(low * NC + core)].astype(F32)
                 + got_c[low, ms, zs].astype(F32)
             ).astype(BF16)
+        there, ms, zs = y_first(c)
+        if there:
+            for s in range(1, ny):
+                low, high = y_peer(s)
+                remote(
+                    acc_c.at[low, ms, zs, :, high], got_y.at[y_at, ms, zs],
+                    send_g.at[1, c], recv_g.at[1, c], *y_peers[s - 1],
+                ).start()
+        ms, zs = x_first(c)
+        for s in range(1, NX):
+            remote(
+                acc_c.at[:, ms, zs, (x + s) % NX], got_xf.at[x, :, ms, zs],
+                send_g.at[2, c], recv_g.at[2, c], *x_peers[s - 1],
+            ).start()
+
+    def second_start(c):
+        there, ms, zs = y_first(c)
+        if there:
+            landed(got_y.at[: ny - 1, ms, zs], recv_g.at[1, c], grp, trk)
+            total = acc_c[y_lo, ms, zs, :, y_hi].astype(F32)
+            for s in range(1, ny):
+                low, high = y_peer(s)
+                total += got_y[high * NYL + low, ms, zs].astype(F32)
+            acc_y[ms, zs] = total.astype(BF16)
+            for s in range(1, NX):
+                remote(
+                    acc_y.at[ms, zs, (x + s) % NX], got_x.at[x, ms, zs],
+                    send_g.at[3, c], recv_g.at[3, c], *x_peers[s - 1],
+                ).start()
+        ms, zs = x_first(c)
+        landed(got_xf.at[: NX - 1, :, ms, zs], recv_g.at[2, c], grp, trk)
+        total = acc_c[:, ms, zs, x].astype(F32)
+        for s in range(1, NX):
+            total += got_xf[(x + s) % NX, :, ms, zs].astype(F32)
+        acc_xf[:, ms, zs] = total.astype(BF16)
         for s in range(1, ny):
             low, high = y_peer(s)
             remote(
-                acc_c.at[low, ms, zs, :, high], got_y.at[y_at, ms, zs],
-                send_g.at[1, c], recv_g.at[1, c], *y_peers[s - 1],
+                acc_xf.at[low, ms, zs, high], got_yl.at[y_at, ms, zs],
+                send_g.at[4, c], recv_g.at[4, c], *y_peers[s - 1],
             ).start()
 
-    def y_finish(c):
-        ms, zs = chunk(c)
-        landed(got_y.at[: ny - 1, ms, zs], recv_g.at[1, c], grp, trk)
-        total = acc_c[y_lo, ms, zs, :, y_hi].astype(F32)
+    def second_finish(c):
+        there, ms, zs = y_first(c)
+        if there:
+            landed(got_x.at[: NX - 1, ms, zs], recv_g.at[3, c], grp, trk)
+            total = acc_y[ms, zs, x].astype(F32)
+            for s in range(1, NX):
+                total += got_x[(x + s) % NX, ms, zs].astype(F32)
+            acc[ms, zs] = total.astype(BF16)
+        ms, zs = x_first(c)
+        landed(got_yl.at[: ny - 1, ms, zs], recv_g.at[4, c], grp, trk)
+        total = acc_xf[y_lo, ms, zs, y_hi].astype(F32)
         for s in range(1, ny):
             low, high = y_peer(s)
-            total += got_y[high * NYL + low, ms, zs].astype(F32)
-        acc_y[ms, zs] = total.astype(BF16)
-        for s in range(1, NX):
-            remote(
-                acc_y.at[ms, zs, (x + s) % NX], got_x.at[x, ms, zs],
-                send_g.at[2, c], recv_g.at[2, c], *x_peers[s - 1],
-            ).start()
-
-    def x_finish(c):
-        ms, zs = chunk(c)
-        landed(got_x.at[: NX - 1, ms, zs], recv_g.at[2, c], grp, trk)
-        total = acc_y[ms, zs, x].astype(F32)
-        for s in range(1, NX):
-            total += got_x[(x + s) % NX, ms, zs].astype(F32)
-        acc_x[ms, zs] = total.astype(BF16)
+            total += got_yl[high * NYL + low, ms, zs].astype(F32)
+        acc[ms, zs] = total.astype(BF16)
 
     raw_tiles = raw.shape[2:]
 
-    exchanged(u_ref, ur, 1)
+    exchanged(us, ur, 1)
     up[...] = ur[...].astype(F32).reshape(length, width).astype(BF16)
     take_weights(3)
     gar[...] = dot(up[...], wt[3], 1, 0).astype(BF16)
@@ -277,10 +335,8 @@
             raw[m, zs] = piece.reshape((zs.stop - zs.start,) + raw_tiles).astype(BF16)
         core_start(pair + 1)
         core_finish(pair)
-        if pair >= 1:
-            y_finish(pair - 1)
         if pair >= 2:
-            x_finish(pair - 2)
+            second_start(pair - 2)
     grad_normed = (
         dot(gqr[...], wt[0], 1, 0) + dot(gkr[...], wt[1], 1, 0) + dot(gvr[...], wt[2], 1, 0)
     )
@@ -294,14 +350,16 @@
         - jnp.mean(scaled, -1, keepdims=True)
         - centred * jnp.mean(scaled * centred, -1, keepdims=True)
     )
+    grad = up[...].astype(F32) + grad.astype(BF16).astype(F32)
     branch[...] = grad.reshape(tracks, cells, width).astype(BF16)
     landed(sum_c.at[0], recv_s.at[0], grp, trk)
     sum_y[y_at] = sum_c[0] + sum_c[1]
     for peer in y_peers:
         remote(sum_y.at[y_at], sum_y.at[y_at], send_s.at[1], recv_s.at[1], *peer).start()
     exchange(branch, out_ref, 2, 0, NZ // 2)
-    y_finish(pairs - 1)
-    x_finish(pairs - 2)
+    for c in range(pairs - 2, pairs):
+        second_start(c)
+    exchange(branch, out_ref, 2, NZ // 2, NZ)
     landed(sum_y.at[: ny - 1], recv_s.at[1], grp, trk)
     all_y = sum_y[0]
     for s in range(1, ny):
@@ -309,13 +367,12 @@
     sum_x[x] = all_y
     for peer in x_peers:
         remote(sum_x.at[x], sum_x.at[x], send_s.at[2], recv_s.at[2], *peer).start()
-    y_finish(pairs)
-    exchange(branch, out_ref, 2, NZ // 2, NZ)
-    x_finish(pairs - 1)
-    x_finish(pairs)
+    second_start(pairs)
+    for c in range(pairs + 1):
+        second_finish(c)
     for s in range(1, NZ):
         remote(
-            acc_x.at[:, (z + s) % NZ], got_z.at[z], send_g.at[3, 0], recv_g.at[3, 0],
+            acc.at[:, (z + s) % NZ], got_z.at[z], send_g.at[5, 0], recv_g.at[5, 0],
             *z_peers[s - 1],
         ).start()
     landed(sum_x.at[: NX - 1], recv_s.at[2], grp, trk)
@@ -325,31 +382,38 @@
     sum_z[z] = all_x
     for peer in z_peers:
         remote(sum_z.at[z], sum_z.at[z], send_s.at[3], recv_s.at[3], *peer).start()
-    landed(got_z.at[: NZ - 1], recv_g.at[3, 0], grp, trk)
-    total = acc_x[:, z].astype(F32)
+    landed(got_z.at[: NZ - 1], recv_g.at[5, 0], grp, trk)
+    total = acc[:, z].astype(F32)
     for s in range(1, NZ):
         total += got_z[(z + s) % NZ].astype(F32)
-    gw_ref[...] = total
+    factor = float(length * lax.axis_size("grp") * tracks) ** (-0.5)
+    gw_ref[...] = total * factor
     landed(sum_z.at[: NZ - 1], recv_s.at[3], grp, trk)
     all_z = sum_z[0]
     for s in range(1, NZ):
         all_z += sum_z[s]
-    gg_ref[...] = all_z
+    gg_ref[...] = all_z * factor
     exchanged(branch, out_ref, 2)
 
     for at in range(3):
         left(out_ref.at[: tracks - 1], send_a.at[at], grp, trk)
     left(wf.at[:, : NZ - 1, 0, 0, :, :128], send_w.at[0], grp, trk)
-    left(wf.at[:, :, : NX - 1, 0, :, :128], send_w.at[1], grp, trk)
+    left(wf.at[:2, :, : NX - 1, 0, :, :128], send_w.at[1], grp, trk)
+    left(wf.at[2:, :, 0, 0, :, : (ny - 1) * 128], send_w.at[10], grp, trk)
     for m in range(4):
-        left(wf.at[m, :, :, 0, :, : (ny - 1) * 128], send_w.at[2 + m], grp, trk)
+        left(last_stage(m), send_w.at[2 + m], grp, trk)
         left(wf.at[m, :, :, :, :, : NYL * 128], send_w.at[6 + m], grp, trk)
     for c in range(pairs + 1):
         ms, zs = chunk(c)
         left(got_c.at[:, ms, zs], send_g.at[0, c], grp, trk)
-        left(got_y.at[: ny - 1, ms, zs], send_g.at[1, c], grp, trk)
-        left(got_x.at[: NX - 1, ms, zs], send_g.at[2, c], grp, trk)
-    left(got_z.at[: NZ - 1], send_g.at[3, 0], grp, trk)
+        there, ms, zs = y_first(c)
+        if there:
+            left(got_y.at[: ny - 1, ms, zs], send_g.at[1, c], grp, trk)
+            left(got_x.at[: NX - 1, ms, zs], send_g.at[3, c], grp, trk)
+        ms, zs = x_first(c)
+        left(got_xf.at[: NX - 1, :, ms, zs], send_g.at[2, c], grp, trk)
+        left(got_yl.at[: ny - 1, ms, zs], send_g.at[4, c], grp, trk)
+    left(got_z.at[: NZ - 1], send_g.at[5, 0], grp, trk)
     left(sum_c.at[0], send_s.at[0], grp, trk)
     left(sum_y.at[: ny - 1], send_s.at[1], grp, trk)
     left(sum_x.at[: NX - 1], send_s.at[2], grp, trk)
@@ -377,6 +441,8 @@
         scratch_shapes=[
             row,
             row,
+            row,
+            row,
             pltpu.VMEM((4, NZ, NX, NYH, outs, width), BF16),
             pltpu.VMEM((4, width, width), BF16),
             pltpu.VMEM((length, width), F32),
@@ -392,20 +458,22 @@
             pltpu.VMEM((ny, 4, NZ, NX, outs, 128), BF16),
             pltpu.VMEM((4, NZ, NX, outs, 128), BF16),
             pltpu.VMEM((NX, 4, NZ, outs, 128), BF16),
+            pltpu.VMEM((NX, NYL, 4, NZ, NYH, outs, 128), BF16),
+            pltpu.VMEM((NYL, 4, NZ, NYH, outs, 128), BF16),
+            pltpu.VMEM((ny, 4, NZ, outs, 128), BF16),
             pltpu.VMEM((4, NZ, outs, 128), BF16),
             pltpu.VMEM((NZ, 4, outs, 128), BF16),
             pltpu.VMEM((NC, 1, width), F32),
             pltpu.VMEM((ny, 1, width), F32),
             pltpu.VMEM((NX, 1, width), F32),
             pltpu.VMEM((NZ, 1, width), F32),
-            pltpu.SemaphoreType.REGULAR((2,)),
+            dma((5,)),
             dma((3,)),
             dma((3,)),
-            dma((3,)),
-            dma((10,)),
-            dma((10,)),
-            dma((4, 5)),
-            dma((4, 5)),
+            dma((11,)),
+            dma((11,)),
+            dma((6, 5)),
+            dma((6, 5)),
             dma((4,)),
             dma((4,)),
         ],
@@ -418,15 +486,11 @@
 
 def shards(fields, upstream, ln_gain, weights):
     tracks, cells, width = fields.shape
-    cell_count = tracks * lax.axis_size("grp") * cells * lax.axis_size("trk")
     w_tile = jnp.swapaxes(weights, 1, 2)
-    branch, raw_part, gain_sum = layer_back(fields, upstream, w_tile, ln_gain.reshape(1, width))
-    factor = float(cell_count) ** (-0.5)
-    return (
-        (upstream.astype(F32) + branch.astype(F32)).astype(BF16),
-        jnp.swapaxes(raw_part, 1, 2) * factor,
-        gain_sum.reshape(width) * factor,
+    grad_fields, grad_tile, grad_gain = layer_back(
+        fields, upstream, w_tile, ln_gain.reshape(1, width)
     )
+    return grad_fields, jnp.swapaxes(grad_tile, 1, 2), grad_gain.reshape(width)
 
 
 def solution(mesh):

time: 94.1 us -> 81.5 us (0.87)
  Pallas kernels: 89.4 us -> 76.6 us
  other arithmetic: 3.16 us -> 0 us
  local copies, waits for them, and re-layouts: 0.01 us -> 3.14 us
    pallas_call x1, Pallas kernels: 89.4 us -> 76.6 us  [layer_back(): pl.pallas_call(row_kernel, out_shape=(jax.ShapeDtypeStruct((tracks, cells...]
    unnamed x6 -> x7, local copies, waits for them, and re-layouts: 0.01 us -> 3.14 us
    convert_element_type x1 -> x0, other arithmetic: 1.97 us -> none  [shards(): (upstream.astype(F32) + branch.astype(F32)).astype(BF16)]
    mul x2 -> x0, other arithmetic: 1.19 us -> none  [the longest x1 0.61 us: shards(): jnp.swapaxes(raw_part, 1, 2) * factor]
where the time goes in v3:
time: 81.5 us; the launch traced here: 80.4 us
  Pallas kernels  76.6 us (94%)
  local copies, waits for them, and re-layouts  3.14 us (4%)
    pallas_call x1, Pallas kernels, layer_back(): pl.pallas_call(row_kernel, out_shape=(jax.ShapeDtypeStruct((tracks, cells...  76.6 us
    unnamed x7, local copies, waits for them, and re-layouts  3.14 us

profile of v3, /device:TPU:2, one launch (start us, length us, event | category | flops | bytes accessed | tf_op | source)
XLA Modules:
  0.0 80.4 jit_solution(724694290369762569)
XLA Ops:
  0.6 76.6 %layer_back.1 = (bf16[64,8,512]{2,1,0:T(8,128)(2,1)}, f32[4,8,128]{2,1,0:T(8,128)}, f32[1,512]{1,0:T(1,128)}) custom-call(bf16[64,8,512]{2,1,0:T(8,128)(2,1)} %f_ref.1, bf16[64,8,512]{2,1,0:T(8,128)(2,1)} %u_ref.1, bf16[4,8,128]{2,1,0:T(8,128)(2,1)} %bitcast.5, f32[1,512]{1,0:T(1,128)} %bitcast.6), custom_call_target="tpu_custom_call" | custom-call | tf_op jit(solution)/shard_map/layer_back/pallas_call | solution.py:432
  77.2 0.0 copy-start
  77.2 1.9 %copy.10 = bf16[64,8,512]{2,1,0:T(8,128)(2,1)} copy(bf16[64,8,512]{2,1,0:T(8,128)(2,1)} %get-tuple-element.12) | data formatting | bytes 1048576
  79.1 0.0 copy-done
  79.1 0.0 copy-start.1
  79.1 0.6 copy.11
  79.7 0.1 copy-done.1
  79.8 0.6 copy.12
Async XLA Ops:
  77.2 1.9 %copy-start = (f32[4,8,128]{2,1,0:T(8,128)S(1)}, f32[4,8,128]{2,1,0:T(8,128)}, u32[]{:S(2)}) copy-start(f32[4,8,128]{2,1,0:T(8,128)} %get-tuple-element.7) | copy-start | bytes 49156
  79.1 0.7 copy-start.1

commit v4 on v3

--- a/solution.py
+++ b/solution.py
@@ -191,7 +191,7 @@
     cen_ref[...] = centred
     inv_ref[...] = inv_std
     nor[...] = (centred * gain).astype(BF16)
-    scaling = HEAD ** (-0.5)
+    scaling = jnp.asarray(HEAD ** (-0.5), BF16)
     for m, ref in ((0, qr), (2, vr), (1, kr)):
         take_weights(m)
         ref[...] = dot(nor[...], wt[m], 1, 1).astype(BF16)
@@ -202,12 +202,12 @@
 
     def forward(pair, carry):
         cols = lanes(pair)
-        q, k, v = qr[:, cols], kr[:, cols], vr[:, cols]
+        q, k, v = qr[:, cols] * scaling, kr[:, cols], vr[:, cols]
         for part in range(2):
             rows = slice(part * half, (part + 1) * half)
             sum_o = jnp.zeros((half, 128), F32)
             for h in range(2):
-                scores = dot(k * masks[h], q[rows], 1, 1) * scaling
+                scores = dot(k * masks[h], q[rows], 1, 1)
                 shifted = jnp.exp(scores - jnp.max(scores, 0, keepdims=True))
                 prob = shifted * (1.0 / jnp.sum(shifted, 0, keepdims=True))
                 prob_ref[2 * pair + h, part] = prob
@@ -313,6 +313,7 @@
     for pair in range(pairs):
         cols = slice(pair * 128, (pair + 1) * 128)
         q, k, v, ga = qr[:, cols], kr[:, cols], vr[:, cols], gar[:, cols]
+        scaled_ga = ga * scaling
         sum_k = jnp.zeros((length, 128), F32)
         sum_v = jnp.zeros((length, 128), F32)
         for part in range(2):
@@ -320,9 +321,9 @@
             sum_q = jnp.zeros((half, 128), F32)
             for h in range(2):
                 prob = prob_ref[2 * pair + h, part]
-                dprobs = dot(v * masks[h], ga[rows], 1, 1)
+                dprobs = dot(v * masks[h], scaled_ga[rows], 1, 1)
                 row_dot = jnp.sum(prob * dprobs, 0, keepdims=True)
-                grad = (prob * (dprobs - row_dot) * scaling).astype(BF16)
+                grad = (prob * (dprobs - row_dot)).astype(BF16)
                 sum_q += dot(grad, k * masks[h], 0, 0)
                 sum_v += dot(prob.astype(BF16), ga[rows] * masks[h], 1, 0)
                 sum_k += dot(grad, q[rows] * masks[h], 1, 0)
@@ -344,6 +345,11 @@
     sum_c[core] = jnp.sum(grad_normed * centred, 0, keepdims=True)
     remote(sum_c.at[core], sum_c.at[core], send_s.at[0], recv_s.at[0], sibling, trk).start()
     core_finish(pairs)
+    second_start(pairs - 2)
+    landed(sum_c.at[0], recv_s.at[0], grp, trk)
+    sum_y[y_at] = sum_c[0] + sum_c[1]
+    for peer in y_peers:
+        remote(sum_y.at[y_at], sum_y.at[y_at], send_s.at[1], recv_s.at[1], *peer).start()
     scaled = grad_normed * gain
     grad = inv_ref[...] * (
         scaled
@@ -352,14 +358,8 @@
     )
     grad = up[...].astype(F32) + grad.astype(BF16).astype(F32)
     branch[...] = grad.reshape(tracks, cells, width).astype(BF16)
-    landed(sum_c.at[0], recv_s.at[0], grp, trk)
-    sum_y[y_at] = sum_c[0] + sum_c[1]
-    for peer in y_peers:
-        remote(sum_y.at[y_at], sum_y.at[y_at], send_s.at[1], recv_s.at[1], *peer).start()
-    exchange(branch, out_ref, 2, 0, NZ // 2)
-    for c in range(pairs - 2, pairs):
-        second_start(c)
-    exchange(branch, out_ref, 2, NZ // 2, NZ)
+    exchange(branch, out_ref, 2, 0, NZ * 3 // 8)
+    second_start(pairs - 1)
     landed(sum_y.at[: ny - 1], recv_s.at[1], grp, trk)
     all_y = sum_y[0]
     for s in range(1, ny):
@@ -368,6 +368,7 @@
     for peer in x_peers:
         remote(sum_x.at[x], sum_x.at[x], send_s.at[2], recv_s.at[2], *peer).start()
     second_start(pairs)
+    exchange(branch, out_ref, 2, NZ * 3 // 8, NZ * 6 // 8)
     for c in range(pairs + 1):
         second_finish(c)
     for s in range(1, NZ):
@@ -382,6 +383,7 @@
     sum_z[z] = all_x
     for peer in z_peers:
         remote(sum_z.at[z], sum_z.at[z], send_s.at[3], recv_s.at[3], *peer).start()
+    exchange(branch, out_ref, 2, NZ * 6 // 8, NZ)
     landed(got_z.at[: NZ - 1], recv_g.at[5, 0], grp, trk)
     total = acc[:, z].astype(F32)
     for s in range(1, NZ):

time: 81.5 us -> 83.1 us (1.020)
  Pallas kernels: 76.6 us -> 78.9 us
    pallas_call x1, Pallas kernels: 76.6 us -> 78.9 us  [layer_back(): pl.pallas_call(row_kernel, out_shape=(jax.ShapeDtypeStruct((tracks, cells...]
where the time goes in v4:
time: 83.1 us; the launch traced here: 82.7 us
  Pallas kernels  78.9 us (95%)
  local copies, waits for them, and re-layouts  3.14 us (4%)
    pallas_call x1, Pallas kernels, layer_back(): pl.pallas_call(row_kernel, out_shape=(jax.ShapeDtypeStruct((tracks, cells...  78.9 us
    unnamed x7, local copies, waits for them, and re-layouts  3.14 us

profile of v4, /device:TPU:2, one launch (start us, length us, event | category | flops | bytes accessed | tf_op | source)
XLA Modules:
  0.0 82.7 jit_solution(6279418448299038318)
XLA Ops:
  0.6 78.9 %layer_back.1 = (bf16[64,8,512]{2,1,0:T(8,128)(2,1)}, f32[4,8,128]{2,1,0:T(8,128)}, f32[1,512]{1,0:T(1,128)}) custom-call(bf16[64,8,512]{2,1,0:T(8,128)(2,1)} %f_ref.1, bf16[64,8,512]{2,1,0:T(8,128)(2,1)} %u_ref.1, bf16[4,8,128]{2,1,0:T(8,128)(2,1)} %bitcast.5, f32[1,512]{1,0:T(1,128)} %bitcast.6), custom_call_target="tpu_custom_call" | custom-call | tf_op jit(solution)/shard_map/layer_back/pallas_call | solution.py:434
  79.6 0.0 copy-start
  79.6 1.9 %copy.10 = bf16[64,8,512]{2,1,0:T(8,128)(2,1)} copy(bf16[64,8,512]{2,1,0:T(8,128)(2,1)} %get-tuple-element.12) | data formatting | bytes 1048576
  81.5 0.0 copy-done
  81.5 0.0 copy-start.1
  81.5 0.6 copy.11
  82.1 0.1 copy-done.1
  82.1 0.6 copy.12
Async XLA Ops:
  79.6 1.9 %copy-start = (f32[4,8,128]{2,1,0:T(8,128)S(1)}, f32[4,8,128]{2,1,0:T(8,128)}, u32[]{:S(2)}) copy-start(f32[4,8,128]{2,1,0:T(8,128)} %get-tuple-element.7) | copy-start | bytes 49156
  81.5 0.7 copy-start.1

commit v5 on v4

--- a/solution.py
+++ b/solution.py
@@ -55,8 +55,8 @@
     f_ref, u_ref, w_ref, gain_ref, out_ref, gw_ref, gg_ref,
     fs, us, fr, ur, wf, wt, cen_ref, inv_ref, prob_ref,
     up, nor, qr, kr, vr, gar, atr, gqr, gkr, gvr, branch,
-    raw, got_c, acc_c, got_y, acc_y, got_x, got_xf, acc_xf, got_yl, acc, got_z,
-    sum_c, sum_y, sum_x, sum_z,
+    raw, got_c, acc_c, got_y, acc_y, got_x, got_xf, acc_xf, got_yl, got_d, acc, got_z,
+    sum_c, sum_y, sum_z,
     local, send_a, recv_a, send_w, recv_w, send_g, recv_g, send_s, recv_s,
 ):
     grp, trk, z, x, y_hi, y_lo, core = position()
@@ -77,6 +77,15 @@
         low, high = y_peer(s)
         y_peers.append((low * NC + core, trk_of(z, x, high)))
 
+    xy_at = y_at * NX + x
+    plane_peers = []
+    for s in range(ny):
+        low, high = y_peer(s)
+        for far in range(NX):
+            if s + far > 0:
+                at_x = (x + far) % NX
+                plane_peers.append((low, high, at_x, (low * NC + core, trk_of(z, at_x, high))))
+
     loads = [
         pltpu.make_async_copy(src, dst, local.at[3 + i])
         for i, (src, dst) in enumerate(((f_ref, fs), (u_ref, us)))
@@ -96,10 +105,11 @@
 
     lax.fori_loop(0, tracks // 2, greet, 0)
     lax.fori_loop(tracks // 2 + 1, tracks, greet, 0)
-    for peer in y_peers:
-        pl.semaphore_signal(barrier, inc=1, device_id=peer, device_id_type=MESH)
+    for k in range(plane):
+        to = ((1 - y_lo) * NC + core, z * plane + k)
+        pl.semaphore_signal(barrier, inc=1, device_id=to, device_id_type=MESH)
     pl.semaphore_signal(barrier, inc=1, device_id=(sibling, trk), device_id_type=MESH)
-    pl.semaphore_wait(barrier, tracks - 1 + len(y_peers) + 1)
+    pl.semaphore_wait(barrier, tracks - 1 + plane + 1)
 
     for peer in z_peers:
         remote(w_ref, mine, send_w.at[0], recv_w.at[0], *peer).start()
@@ -198,21 +208,28 @@
     half = length // 2
     lane = lax.broadcasted_iota(jnp.int32, (1, 128), 1)
     masks = [((lane >= h * HEAD) & (lane < (h + 1) * HEAD)).astype(BF16) for h in range(2)]
+    turned = lax.broadcasted_iota(jnp.int32, (128, 1), 0)
+    turned_masks = [
+        ((turned >= h * HEAD) & (turned < (h + 1) * HEAD)).astype(BF16) for h in range(2)
+    ]
     pairs = width // 128
 
     def forward(pair, carry):
         cols = lanes(pair)
         q, k, v = qr[:, cols] * scaling, kr[:, cols], vr[:, cols]
+        v_turned = v.T
+        k_of = [k * masks[h] for h in range(2)]
+        v_of = [v_turned * turned_masks[h] for h in range(2)]
         for part in range(2):
             rows = slice(part * half, (part + 1) * half)
-            sum_o = jnp.zeros((half, 128), F32)
+            sum_o = jnp.zeros((128, half), F32)
             for h in range(2):
-                scores = dot(k * masks[h], q[rows], 1, 1)
+                scores = dot(k_of[h], q[rows], 1, 1)
                 shifted = jnp.exp(scores - jnp.max(scores, 0, keepdims=True))
                 prob = shifted * (1.0 / jnp.sum(shifted, 0, keepdims=True))
                 prob_ref[2 * pair + h, part] = prob
-                sum_o += dot(prob.astype(BF16), v * masks[h], 0, 0)
-            atr[rows, cols] = sum_o.astype(BF16)
+                sum_o += dot(v_of[h], prob.astype(BF16), 1, 0)
+            atr[rows, cols] = sum_o.T.astype(BF16)
         return carry
 
     lax.fori_loop(0, pairs, forward, 0)
@@ -244,6 +261,13 @@
                 raw[ms, zs, :, :, :, lanes(low * NC + core)].astype(F32)
                 + got_c[low, ms, zs].astype(F32)
             ).astype(BF16)
+        if c == pairs:
+            for low, high, at_x, to in plane_peers:
+                remote(
+                    acc_c.at[low, ms, zs, at_x, high], got_d.at[xy_at],
+                    send_g.at[1, c], recv_g.at[1, c], *to,
+                ).start()
+            return
         there, ms, zs = y_first(c)
         if there:
             for s in range(1, ny):
@@ -286,6 +310,14 @@
                 send_g.at[4, c], recv_g.at[4, c], *y_peers[s - 1],
             ).start()
 
+    def direct_finish(c):
+        ms, zs = chunk(c)
+        landed(got_d.at[: ny * NX - 1], recv_g.at[1, c], grp, trk)
+        total = acc_c[y_lo, ms, zs, x, y_hi].astype(F32)
+        for low, high, at_x, _ in plane_peers:
+            total += got_d[(high * NYL + low) * NX + at_x].astype(F32)
+        acc[ms, zs] = total.astype(BF16)
+
     def second_finish(c):
         there, ms, zs = y_first(c)
         if there:
@@ -314,42 +346,50 @@
         cols = slice(pair * 128, (pair + 1) * 128)
         q, k, v, ga = qr[:, cols], kr[:, cols], vr[:, cols], gar[:, cols]
         scaled_ga = ga * scaling
+        k_turned = k.T
+        k_of = [k_turned * turned_masks[h] for h in range(2)]
+        v_of = [v * masks[h] for h in range(2)]
+        q_of = [q * masks[h] for h in range(2)]
+        ga_of = [ga * masks[h] for h in range(2)]
         sum_k = jnp.zeros((length, 128), F32)
         sum_v = jnp.zeros((length, 128), F32)
         for part in range(2):
             rows = slice(part * half, (part + 1) * half)
-            sum_q = jnp.zeros((half, 128), F32)
+            sum_q = jnp.zeros((128, half), F32)
             for h in range(2):
                 prob = prob_ref[2 * pair + h, part]
-                dprobs = dot(v * masks[h], scaled_ga[rows], 1, 1)
+                dprobs = dot(v_of[h], scaled_ga[rows], 1, 1)
                 row_dot = jnp.sum(prob * dprobs, 0, keepdims=True)
                 grad = (prob * (dprobs - row_dot)).astype(BF16)
-                sum_q += dot(grad, k * masks[h], 0, 0)
-                sum_v += dot(prob.astype(BF16), ga[rows] * masks[h], 1, 0)
-                sum_k += dot(grad, q[rows] * masks[h], 1, 0)
-            gqr[rows, cols] = sum_q.astype(BF16)
+                sum_q += dot(k_of[h], grad, 1, 0)
+                sum_v += dot(prob.astype(BF16), ga_of[h][rows], 1, 0)
+                sum_k += dot(grad, q_of[h][rows], 1, 0)
+            gqr[cols, rows] = sum_q.astype(BF16)
         gkr[:, cols] = sum_k.astype(BF16)
         gvr[:, cols] = sum_v.astype(BF16)
         zs = chunk(pair + 1)[1]
-        for m, ref in enumerate((gqr, gkr, gvr)):
-            piece = dot(ref[:, cols], nor[...], 0, 0)
+        for m, piece in enumerate((
+            dot(gqr[cols, :], nor[...], 1, 0),
+            dot(gkr[:, cols], nor[...], 0, 0),
+            dot(gvr[:, cols], nor[...], 0, 0),
+        )):
             raw[m, zs] = piece.reshape((zs.stop - zs.start,) + raw_tiles).astype(BF16)
         core_start(pair + 1)
         core_finish(pair)
         if pair >= 2:
             second_start(pair - 2)
     grad_normed = (
-        dot(gqr[...], wt[0], 1, 0) + dot(gkr[...], wt[1], 1, 0) + dot(gvr[...], wt[2], 1, 0)
+        dot(gqr[...], wt[0], 0, 0) + dot(gkr[...], wt[1], 1, 0) + dot(gvr[...], wt[2], 1, 0)
     )
     centred = cen_ref[...]
     sum_c[core] = jnp.sum(grad_normed * centred, 0, keepdims=True)
     remote(sum_c.at[core], sum_c.at[core], send_s.at[0], recv_s.at[0], sibling, trk).start()
     core_finish(pairs)
+    landed(sum_c.at[0], recv_s.at[0], grp, trk)
+    sum_y[xy_at] = sum_c[0] + sum_c[1]
+    for _, _, _, to in plane_peers:
+        remote(sum_y.at[xy_at], sum_y.at[xy_at], send_s.at[1], recv_s.at[1], *to).start()
     second_start(pairs - 2)
-    landed(sum_c.at[0], recv_s.at[0], grp, trk)
-    sum_y[y_at] = sum_c[0] + sum_c[1]
-    for peer in y_peers:
-        remote(sum_y.at[y_at], sum_y.at[y_at], send_s.at[1], recv_s.at[1], *peer).start()
     scaled = grad_normed * gain
     grad = inv_ref[...] * (
         scaled
@@ -358,32 +398,24 @@
     )
     grad = up[...].astype(F32) + grad.astype(BF16).astype(F32)
     branch[...] = grad.reshape(tracks, cells, width).astype(BF16)
-    exchange(branch, out_ref, 2, 0, NZ * 3 // 8)
     second_start(pairs - 1)
-    landed(sum_y.at[: ny - 1], recv_s.at[1], grp, trk)
-    all_y = sum_y[0]
-    for s in range(1, ny):
-        all_y += sum_y[s]
-    sum_x[x] = all_y
-    for peer in x_peers:
-        remote(sum_x.at[x], sum_x.at[x], send_s.at[2], recv_s.at[2], *peer).start()
-    second_start(pairs)
-    exchange(branch, out_ref, 2, NZ * 3 // 8, NZ * 6 // 8)
-    for c in range(pairs + 1):
+    exchange(branch, out_ref, 2, 0, NZ * 5 // 8)
+    direct_finish(pairs)
+    for c in range(pairs):
         second_finish(c)
     for s in range(1, NZ):
         remote(
             acc.at[:, (z + s) % NZ], got_z.at[z], send_g.at[5, 0], recv_g.at[5, 0],
             *z_peers[s - 1],
         ).start()
-    landed(sum_x.at[: NX - 1], recv_s.at[2], grp, trk)
-    all_x = sum_x[0]
-    for s in range(1, NX):
-        all_x += sum_x[s]
-    sum_z[z] = all_x
+    landed(sum_y.at[: ny * NX - 1], recv_s.at[1], grp, trk)
+    all_y = sum_y[0]
+    for s in range(1, ny * NX):
+        all_y += sum_y[s]
+    sum_z[z] = all_y
     for peer in z_peers:
         remote(sum_z.at[z], sum_z.at[z], send_s.at[3], recv_s.at[3], *peer).start()
-    exchange(branch, out_ref, 2, NZ * 6 // 8, NZ)
+    exchange(branch, out_ref, 2, NZ * 5 // 8, NZ)
     landed(got_z.at[: NZ - 1], recv_g.at[5, 0], grp, trk)
     total = acc[:, z].astype(F32)
     for s in range(1, NZ):
@@ -408,6 +440,9 @@
     for c in range(pairs + 1):
         ms, zs = chunk(c)
         left(got_c.at[:, ms, zs], send_g.at[0, c], grp, trk)
+        if c == pairs:
+            left(got_d.at[: ny * NX - 1], send_g.at[1, c], grp, trk)
+            break
         there, ms, zs = y_first(c)
         if there:
             left(got_y.at[: ny - 1, ms, zs], send_g.at[1, c], grp, trk)
@@ -417,8 +452,7 @@
         left(got_yl.at[: ny - 1, ms, zs], send_g.at[4, c], grp, trk)
     left(got_z.at[: NZ - 1], send_g.at[5, 0], grp, trk)
     left(sum_c.at[0], send_s.at[0], grp, trk)
-    left(sum_y.at[: ny - 1], send_s.at[1], grp, trk)
-    left(sum_x.at[: NX - 1], send_s.at[2], grp, trk)
+    left(sum_y.at[: ny * NX - 1], send_s.at[1], grp, trk)
     left(sum_z.at[: NZ - 1], send_s.at[3], grp, trk)
 
 
@@ -451,7 +485,9 @@
             pltpu.VMEM((length, 1), F32),
             pltpu.VMEM((width // HEAD, 2, length, length // 2), F32),
         ]
-        + [square] * 10
+        + [square] * 7
+        + [pltpu.VMEM((width, length), BF16)]
+        + [square] * 2
         + [
             row,
             pltpu.VMEM((4, NZ, NX, NYH, outs, width), BF16),
@@ -463,11 +499,11 @@
             pltpu.VMEM((NX, NYL, 4, NZ, NYH, outs, 128), BF16),
             pltpu.VMEM((NYL, 4, NZ, NYH, outs, 128), BF16),
             pltpu.VMEM((ny, 4, NZ, outs, 128), BF16),
+            pltpu.VMEM((ny * NX, 3, NZ * 128 // width, outs, 128), BF16),
             pltpu.VMEM((4, NZ, outs, 128), BF16),
             pltpu.VMEM((NZ, 4, outs, 128), BF16),
             pltpu.VMEM((NC, 1, width), F32),
-            pltpu.VMEM((ny, 1, width), F32),
-            pltpu.VMEM((NX, 1, width), F32),
+            pltpu.VMEM((ny * NX, 1, width), F32),
             pltpu.VMEM((NZ, 1, width), F32),
             dma((5,)),
             dma((3,)),

time: 83.1 us -> 83.1 us (level)
  no operation moved by 1% of the time
where the time goes in v5:
time: 83.1 us; the launch traced here: 82.3 us
  Pallas kernels  78.6 us (95%)
  local copies, waits for them, and re-layouts  3.14 us (4%)
    pallas_call x1, Pallas kernels, layer_back(): pl.pallas_call(row_kernel, out_shape=(jax.ShapeDtypeStruct((tracks, cells...  78.6 us
    unnamed x7, local copies, waits for them, and re-layouts  3.14 us

profile of v5, /device:TPU:2, one launch (start us, length us, event | category | flops | bytes accessed | tf_op | source)
XLA Modules:
  0.0 82.3 jit_solution(12881536871357669476)
XLA Ops:
  0.6 78.6 %layer_back.1 = (bf16[64,8,512]{2,1,0:T(8,128)(2,1)}, f32[4,8,128]{2,1,0:T(8,128)}, f32[1,512]{1,0:T(1,128)}) custom-call(bf16[64,8,512]{2,1,0:T(8,128)(2,1)} %f_ref.1, bf16[64,8,512]{2,1,0:T(8,128)(2,1)} %u_ref.1, bf16[4,8,128]{2,1,0:T(8,128)(2,1)} %bitcast.5, f32[1,512]{1,0:T(1,128)} %bitcast.6), custom_call_target="tpu_custom_call" | custom-call | tf_op jit(solution)/shard_map/layer_back/pallas_call | solution.py:468
  79.2 0.0 copy-start
  79.2 1.9 %copy.10 = bf16[64,8,512]{2,1,0:T(8,128)(2,1)} copy(bf16[64,8,512]{2,1,0:T(8,128)(2,1)} %get-tuple-element.12) | data formatting | bytes 1048576
  81.1 0.0 copy-done
  81.1 0.0 copy-start.1
  81.1 0.6 copy.11
  81.7 0.1 copy-done.1
  81.8 0.6 copy.12
Async XLA Ops:
  79.2 1.9 %copy-start = (f32[4,8,128]{2,1,0:T(8,128)S(1)}, f32[4,8,128]{2,1,0:T(8,128)}, u32[]{:S(2)}) copy-start(f32[4,8,128]{2,1,0:T(8,128)} %get-tuple-element.7) | copy-start | bytes 49156
  81.1 0.7 copy-start.1

commit v6 on v5

--- a/solution.py
+++ b/solution.py
@@ -55,7 +55,7 @@
     f_ref, u_ref, w_ref, gain_ref, out_ref, gw_ref, gg_ref,
     fs, us, fr, ur, wf, wt, cen_ref, inv_ref, prob_ref,
     up, nor, qr, kr, vr, gar, atr, gqr, gkr, gvr, branch,
-    raw, got_c, acc_c, got_y, acc_y, got_x, got_xf, acc_xf, got_yl, got_d, acc, got_z,
+    raw, got_c, acc_c, got_d, acc, got_z,
     sum_c, sum_y, sum_z,
     local, send_a, recv_a, send_w, recv_w, send_g, recv_g, send_s, recv_s,
 ):
@@ -239,12 +239,6 @@
             return slice(3, 4), slice(0, NZ)
         return slice(0, 3), slice((c - 1) * NZ // pairs, c * NZ // pairs)
 
-    def y_first(c):
-        return c > 0, slice(0, 2), chunk(c)[1]
-
-    def x_first(c):
-        return slice(2, 3) if c > 0 else slice(3, 4), chunk(c)[1]
-
     def core_start(c):
         ms, zs = chunk(c)
         for low in range(NYL):
@@ -261,84 +255,25 @@
                 raw[ms, zs, :, :, :, lanes(low * NC + core)].astype(F32)
                 + got_c[low, ms, zs].astype(F32)
             ).astype(BF16)
-        if c == pairs:
-            for low, high, at_x, to in plane_peers:
-                remote(
-                    acc_c.at[low, ms, zs, at_x, high], got_d.at[xy_at],
-                    send_g.at[1, c], recv_g.at[1, c], *to,
-                ).start()
-            return
-        there, ms, zs = y_first(c)
-        if there:
-            for s in range(1, ny):
-                low, high = y_peer(s)
-                remote(
-                    acc_c.at[low, ms, zs, :, high], got_y.at[y_at, ms, zs],
-                    send_g.at[1, c], recv_g.at[1, c], *y_peers[s - 1],
-                ).start()
-        ms, zs = x_first(c)
-        for s in range(1, NX):
+        for low, high, at_x, to in plane_peers:
             remote(
-                acc_c.at[:, ms, zs, (x + s) % NX], got_xf.at[x, :, ms, zs],
-                send_g.at[2, c], recv_g.at[2, c], *x_peers[s - 1],
+                acc_c.at[low, ms, zs, at_x, high], got_d.at[xy_at, ms, zs],
+                send_g.at[1, c], recv_g.at[1, c], *to,
             ).start()
 
-    def second_start(c):
-        there, ms, zs = y_first(c)
-        if there:
-            landed(got_y.at[: ny - 1, ms, zs], recv_g.at[1, c], grp, trk)
-            total = acc_c[y_lo, ms, zs, :, y_hi].astype(F32)
-            for s in range(1, ny):
-                low, high = y_peer(s)
-                total += got_y[high * NYL + low, ms, zs].astype(F32)
-            acc_y[ms, zs] = total.astype(BF16)
-            for s in range(1, NX):
-                remote(
-                    acc_y.at[ms, zs, (x + s) % NX], got_x.at[x, ms, zs],
-                    send_g.at[3, c], recv_g.at[3, c], *x_peers[s - 1],
-                ).start()
-        ms, zs = x_first(c)
-        landed(got_xf.at[: NX - 1, :, ms, zs], recv_g.at[2, c], grp, trk)
-        total = acc_c[:, ms, zs, x].astype(F32)
-        for s in range(1, NX):
-            total += got_xf[(x + s) % NX, :, ms, zs].astype(F32)
-        acc_xf[:, ms, zs] = total.astype(BF16)
-        for s in range(1, ny):
-            low, high = y_peer(s)
-            remote(
-                acc_xf.at[low, ms, zs, high], got_yl.at[y_at, ms, zs],
-                send_g.at[4, c], recv_g.at[4, c], *y_peers[s - 1],
-            ).start()
-
-    def direct_finish(c):
+    def plane_finish(c):
         ms, zs = chunk(c)
-        landed(got_d.at[: ny * NX - 1], recv_g.at[1, c], grp, trk)
+        landed(got_d.at[: ny * NX - 1, ms, zs], recv_g.at[1, c], grp, trk)
         total = acc_c[y_lo, ms, zs, x, y_hi].astype(F32)
         for low, high, at_x, _ in plane_peers:
-            total += got_d[(high * NYL + low) * NX + at_x].astype(F32)
+            total += got_d[(high * NYL + low) * NX + at_x, ms, zs].astype(F32)
         acc[ms, zs] = total.astype(BF16)
 
-    def second_finish(c):
-        there, ms, zs = y_first(c)
-        if there:
-            landed(got_x.at[: NX - 1, ms, zs], recv_g.at[3, c], grp, trk)
-            total = acc_y[ms, zs, x].astype(F32)
-            for s in range(1, NX):
-                total += got_x[(x + s) % NX, ms, zs].astype(F32)
-            acc[ms, zs] = total.astype(BF16)
-        ms, zs = x_first(c)
-        landed(got_yl.at[: ny - 1, ms, zs], recv_g.at[4, c], grp, trk)
-        total = acc_xf[y_lo, ms, zs, y_hi].astype(F32)
-        for s in range(1, ny):
-            low, high = y_peer(s)
-            total += got_yl[high * NYL + low, ms, zs].astype(F32)
-        acc[ms, zs] = total.astype(BF16)
-
     raw_tiles = raw.shape[2:]
 
+    take_weights(3)
     exchanged(us, ur, 1)
     up[...] = ur[...].astype(F32).reshape(length, width).astype(BF16)
-    take_weights(3)
     gar[...] = dot(up[...], wt[3], 1, 0).astype(BF16)
     raw[3] = dot(up[...], atr[...], 0, 0).reshape(raw.shape[1:]).astype(BF16)
     core_start(0)
@@ -376,8 +311,6 @@
             raw[m, zs] = piece.reshape((zs.stop - zs.start,) + raw_tiles).astype(BF16)
         core_start(pair + 1)
         core_finish(pair)
-        if pair >= 2:
-            second_start(pair - 2)
     grad_normed = (
         dot(gqr[...], wt[0], 0, 0) + dot(gkr[...], wt[1], 1, 0) + dot(gvr[...], wt[2], 1, 0)
     )
@@ -385,11 +318,6 @@
     sum_c[core] = jnp.sum(grad_normed * centred, 0, keepdims=True)
     remote(sum_c.at[core], sum_c.at[core], send_s.at[0], recv_s.at[0], sibling, trk).start()
     core_finish(pairs)
-    landed(sum_c.at[0], recv_s.at[0], grp, trk)
-    sum_y[xy_at] = sum_c[0] + sum_c[1]
-    for _, _, _, to in plane_peers:
-        remote(sum_y.at[xy_at], sum_y.at[xy_at], send_s.at[1], recv_s.at[1], *to).start()
-    second_start(pairs - 2)
     scaled = grad_normed * gain
     grad = inv_ref[...] * (
         scaled
@@ -398,14 +326,16 @@
     )
     grad = up[...].astype(F32) + grad.astype(BF16).astype(F32)
     branch[...] = grad.reshape(tracks, cells, width).astype(BF16)
-    second_start(pairs - 1)
-    exchange(branch, out_ref, 2, 0, NZ * 5 // 8)
-    direct_finish(pairs)
-    for c in range(pairs):
-        second_finish(c)
+    exchange(branch, out_ref, 2, 0, NZ)
+    landed(sum_c.at[0], recv_s.at[0], grp, trk)
+    sum_y[xy_at] = sum_c[0] + sum_c[1]
+    for _, _, _, to in plane_peers:
+        remote(sum_y.at[xy_at], sum_y.at[xy_at], send_s.at[1], recv_s.at[1], *to).start()
+    for c in range(pairs + 1):
+        plane_finish(c)
     for s in range(1, NZ):
         remote(
-            acc.at[:, (z + s) % NZ], got_z.at[z], send_g.at[5, 0], recv_g.at[5, 0],
+            acc.at[:, (z + s) % NZ], got_z.at[z], send_g.at[2, 0], recv_g.at[2, 0],
             *z_peers[s - 1],
         ).start()
     landed(sum_y.at[: ny * NX - 1], recv_s.at[1], grp, trk)
@@ -414,15 +344,14 @@
         all_y += sum_y[s]
     sum_z[z] = all_y
     for peer in z_peers:
-        remote(sum_z.at[z], sum_z.at[z], send_s.at[3], recv_s.at[3], *peer).start()
-    exchange(branch, out_ref, 2, NZ * 5 // 8, NZ)
-    landed(got_z.at[: NZ - 1], recv_g.at[5, 0], grp, trk)
+        remote(sum_z.at[z], sum_z.at[z], send_s.at[2], recv_s.at[2], *peer).start()
+    landed(got_z.at[: NZ - 1], recv_g.at[2, 0], grp, trk)
     total = acc[:, z].astype(F32)
     for s in range(1, NZ):
         total += got_z[(z + s) % NZ].astype(F32)
     factor = float(length * lax.axis_size("grp") * tracks) ** (-0.5)
     gw_ref[...] = total * factor
-    landed(sum_z.at[: NZ - 1], recv_s.at[3], grp, trk)
+    landed(sum_z.at[: NZ - 1], recv_s.at[2], grp, trk)
     all_z = sum_z[0]
     for s in range(1, NZ):
         all_z += sum_z[s]
@@ -440,20 +369,11 @@
     for c in range(pairs + 1):
         ms, zs = chunk(c)
         left(got_c.at[:, ms, zs], send_g.at[0, c], grp, trk)
-        if c == pairs:
-            left(got_d.at[: ny * NX - 1], send_g.at[1, c], grp, trk)
-            break
-        there, ms, zs = y_first(c)
-        if there:
-            left(got_y.at[: ny - 1, ms, zs], send_g.at[1, c], grp, trk)
-            left(got_x.at[: NX - 1, ms, zs], send_g.at[3, c], grp, trk)
-        ms, zs = x_first(c)
-        left(got_xf.at[: NX - 1, :, ms, zs], send_g.at[2, c], grp, trk)
-        left(got_yl.at[: ny - 1, ms, zs], send_g.at[4, c], grp, trk)
-    left(got_z.at[: NZ - 1], send_g.at[5, 0], grp, trk)
+        left(got_d.at[: ny * NX - 1, ms, zs], send_g.at[1, c], grp, trk)
+    left(got_z.at[: NZ - 1], send_g.at[2, 0], grp, trk)
     left(sum_c.at[0], send_s.at[0], grp, trk)
     left(sum_y.at[: ny * NX - 1], send_s.at[1], grp, trk)
-    left(sum_z.at[: NZ - 1], send_s.at[3], grp, trk)
+    left(sum_z.at[: NZ - 1], send_s.at[2], grp, trk)
 
 
 def layer_back(fields, upstream, w_tile, gain):
@@ -493,13 +413,7 @@
             pltpu.VMEM((4, NZ, NX, NYH, outs, width), BF16),
             pltpu.VMEM((NYL, 4, NZ, NX, NYH, outs, 128), BF16),
             pltpu.VMEM((NYL, 4, NZ, NX, NYH, outs, 128), BF16),
-            pltpu.VMEM((ny, 4, NZ, NX, outs, 128), BF16),
-            pltpu.VMEM((4, NZ, NX, outs, 128), BF16),
-            pltpu.VMEM((NX, 4, NZ, outs, 128), BF16),
-            pltpu.VMEM((NX, NYL, 4, NZ, NYH, outs, 128), BF16),
-            pltpu.VMEM((NYL, 4, NZ, NYH, outs, 128), BF16),
-            pltpu.VMEM((ny, 4, NZ, outs, 128), BF16),
-            pltpu.VMEM((ny * NX, 3, NZ * 128 // width, outs, 128), BF16),
+            pltpu.VMEM((ny * NX, 4, NZ, outs, 128), BF16),
             pltpu.VMEM((4, NZ, outs, 128), BF16),
             pltpu.VMEM((NZ, 4, outs, 128), BF16),
             pltpu.VMEM((NC, 1, width), F32),
@@ -510,10 +424,10 @@
             dma((3,)),
             dma((11,)),
             dma((11,)),
-            dma((6, 5)),
-            dma((6, 5)),
-            dma((4,)),
-            dma((4,)),
+            dma((3, 5)),
+            dma((3, 5)),
+            dma((3,)),
+            dma((3,)),
         ],
         compiler_params=pltpu.CompilerParams(
             collective_id=1, has_side_effects=True, vmem_limit_bytes=56 << 20

time: 83.1 us -> 79 us (0.951)
  Pallas kernels: 78.6 us -> 73.9 us
    pallas_call x1, Pallas kernels: 78.6 us -> 73.9 us  [layer_back(): pl.pallas_call(row_kernel, out_shape=(jax.ShapeDtypeStruct((tracks, cells...]
where the time goes in v6:
time: 79 us; the launch traced here: 77.7 us
  Pallas kernels  73.9 us (94%)
  local copies, waits for them, and re-layouts  3.14 us (4%)
    pallas_call x1, Pallas kernels, layer_back(): pl.pallas_call(row_kernel, out_shape=(jax.ShapeDtypeStruct((tracks, cells...  73.9 us
    unnamed x7, local copies, waits for them, and re-layouts  3.14 us

profile of v6, /device:TPU:2, one launch (start us, length us, event | category | flops | bytes accessed | tf_op | source)
XLA Modules:
  0.0 77.7 jit_solution(2053263933043188264)
XLA Ops:
  0.6 73.9 %layer_back.1 = (bf16[64,8,512]{2,1,0:T(8,128)(2,1)}, f32[4,8,128]{2,1,0:T(8,128)}, f32[1,512]{1,0:T(1,128)}) custom-call(bf16[64,8,512]{2,1,0:T(8,128)(2,1)} %f_ref.1, bf16[64,8,512]{2,1,0:T(8,128)(2,1)} %u_ref.1, bf16[4,8,128]{2,1,0:T(8,128)(2,1)} %bitcast.5, f32[1,512]{1,0:T(1,128)} %bitcast.6), custom_call_target="tpu_custom_call" | custom-call | tf_op jit(solution)/shard_map/layer_back/pallas_call | solution.py:388
  74.5 0.0 copy-start
  74.5 1.9 %copy.10 = bf16[64,8,512]{2,1,0:T(8,128)(2,1)} copy(bf16[64,8,512]{2,1,0:T(8,128)(2,1)} %get-tuple-element.12) | data formatting | bytes 1048576
  76.4 0.0 copy-done
  76.4 0.0 copy-start.1
  76.4 0.6 copy.11
  77.0 0.1 copy-done.1
  77.1 0.6 copy.12
Async XLA Ops:
  74.5 1.9 %copy-start = (f32[4,8,128]{2,1,0:T(8,128)S(1)}, f32[4,8,128]{2,1,0:T(8,128)}, u32[]{:S(2)}) copy-start(f32[4,8,128]{2,1,0:T(8,128)} %get-tuple-element.7) | copy-start | bytes 49156
  76.4 0.7 copy-start.1

commit v7 on v5

--- a/solution.py
+++ b/solution.py
@@ -150,6 +150,7 @@
         pltpu.make_async_copy(src.at[trk], dst.at[trk], local.at[min(at, 1)]).wait()
 
     exchange(fs, fr, 0, 0, NZ)
+    exchange(us, ur, 1, 0, NZ)
     own.wait()
     landed(wf.at[:, : NZ - 1, 0, 0, :, :128], recv_w.at[0], grp, trk)
     by_x = wf.at[:2, :, x, y_hi, :, lanes(grp)]
@@ -158,7 +159,6 @@
         remote(by_x, by_x, send_w.at[1], recv_w.at[1], *peer).start()
     for peer in y_peers:
         remote(by_y, by_y, send_w.at[10], recv_w.at[10], *peer).start()
-    exchange(us, ur, 1, 0, NZ // 2)
     landed(wf.at[:2, :, : NX - 1, 0, :, :128], recv_w.at[1], grp, trk)
     landed(wf.at[2:, :, 0, 0, :, : (ny - 1) * 128], recv_w.at[10], grp, trk)
     for m in (0, 2, 1, 3):
@@ -172,7 +172,6 @@
                 part = wf.at[m, :, x, high, :, lanes(low * NC + core)]
                 for peer in x_peers:
                     remote(part, part, send_w.at[2 + m], recv_w.at[2 + m], *peer).start()
-    exchange(us, ur, 1, NZ // 2, NZ)
 
     def last_stage(m):
         if m < 2:
@@ -336,9 +335,9 @@
 
     raw_tiles = raw.shape[2:]
 
+    take_weights(3)
     exchanged(us, ur, 1)
     up[...] = ur[...].astype(F32).reshape(length, width).astype(BF16)
-    take_weights(3)
     gar[...] = dot(up[...], wt[3], 1, 0).astype(BF16)
     raw[3] = dot(up[...], atr[...], 0, 0).reshape(raw.shape[1:]).astype(BF16)
     core_start(0)
@@ -376,8 +375,6 @@
             raw[m, zs] = piece.reshape((zs.stop - zs.start,) + raw_tiles).astype(BF16)
         core_start(pair + 1)
         core_finish(pair)
-        if pair >= 2:
-            second_start(pair - 2)
     grad_normed = (
         dot(gqr[...], wt[0], 0, 0) + dot(gkr[...], wt[1], 1, 0) + dot(gvr[...], wt[2], 1, 0)
     )
@@ -385,11 +382,6 @@
     sum_c[core] = jnp.sum(grad_normed * centred, 0, keepdims=True)
     remote(sum_c.at[core], sum_c.at[core], send_s.at[0], recv_s.at[0], sibling, trk).start()
     core_finish(pairs)
-    landed(sum_c.at[0], recv_s.at[0], grp, trk)
-    sum_y[xy_at] = sum_c[0] + sum_c[1]
-    for _, _, _, to in plane_peers:
-        remote(sum_y.at[xy_at], sum_y.at[xy_at], send_s.at[1], recv_s.at[1], *to).start()
-    second_start(pairs - 2)
     scaled = grad_normed * gain
     grad = inv_ref[...] * (
         scaled
@@ -398,8 +390,13 @@
     )
     grad = up[...].astype(F32) + grad.astype(BF16).astype(F32)
     branch[...] = grad.reshape(tracks, cells, width).astype(BF16)
-    second_start(pairs - 1)
-    exchange(branch, out_ref, 2, 0, NZ * 5 // 8)
+    exchange(branch, out_ref, 2, 0, NZ)
+    landed(sum_c.at[0], recv_s.at[0], grp, trk)
+    sum_y[xy_at] = sum_c[0] + sum_c[1]
+    for _, _, _, to in plane_peers:
+        remote(sum_y.at[xy_at], sum_y.at[xy_at], send_s.at[1], recv_s.at[1], *to).start()
+    for c in range(pairs):
+        second_start(c)
     direct_finish(pairs)
     for c in range(pairs):
         second_finish(c)
@@ -415,7 +412,6 @@
     sum_z[z] = all_y
     for peer in z_peers:
         remote(sum_z.at[z], sum_z.at[z], send_s.at[3], recv_s.at[3], *peer).start()
-    exchange(branch, out_ref, 2, NZ * 5 // 8, NZ)
     landed(got_z.at[: NZ - 1], recv_g.at[5, 0], grp, trk)
     total = acc[:, z].astype(F32)
     for s in range(1, NZ):

time: 83.1 us -> 78.7 us (0.947)
  Pallas kernels: 78.6 us -> 73.5 us
    pallas_call x1, Pallas kernels: 78.6 us -> 73.5 us  [layer_back(): pl.pallas_call(row_kernel, out_shape=(jax.ShapeDtypeStruct((tracks, cells...]
where the time goes in v7:
time: 78.7 us; the launch traced here: 77.3 us
  Pallas kernels  73.5 us (93%)
  local copies, waits for them, and re-layouts  3.14 us (4%)
    pallas_call x1, Pallas kernels, layer_back(): pl.pallas_call(row_kernel, out_shape=(jax.ShapeDtypeStruct((tracks, cells...  73.5 us
    unnamed x7, local copies, waits for them, and re-layouts  3.14 us

profile of v7, /device:TPU:2, one launch (start us, length us, event | category | flops | bytes accessed | tf_op | source)
XLA Modules:
  0.0 77.3 jit_solution(3044979148937747071)
XLA Ops:
  0.6 73.5 %layer_back.1 = (bf16[64,8,512]{2,1,0:T(8,128)(2,1)}, f32[4,8,128]{2,1,0:T(8,128)}, f32[1,512]{1,0:T(1,128)}) custom-call(bf16[64,8,512]{2,1,0:T(8,128)(2,1)} %f_ref.1, bf16[64,8,512]{2,1,0:T(8,128)(2,1)} %u_ref.1, bf16[4,8,128]{2,1,0:T(8,128)(2,1)} %bitcast.5, f32[1,512]{1,0:T(1,128)} %bitcast.6), custom_call_target="tpu_custom_call" | custom-call | tf_op jit(solution)/shard_map/layer_back/pallas_call | solution.py:464
  74.1 0.0 copy-start
  74.1 1.9 %copy.10 = bf16[64,8,512]{2,1,0:T(8,128)(2,1)} copy(bf16[64,8,512]{2,1,0:T(8,128)(2,1)} %get-tuple-element.12) | data formatting | bytes 1048576
  76.0 0.0 copy-done
  76.0 0.0 copy-start.1
  76.0 0.6 copy.11
  76.6 0.1 copy-done.1
  76.7 0.6 copy.12
Async XLA Ops:
  74.1 1.9 %copy-start = (f32[4,8,128]{2,1,0:T(8,128)S(1)}, f32[4,8,128]{2,1,0:T(8,128)}, u32[]{:S(2)}) copy-start(f32[4,8,128]{2,1,0:T(8,128)} %get-tuple-element.7) | copy-start | bytes 49156
  76.0 0.7 copy-start.1
